TPU v7x, 128 devices: a whole 4x4x4 slice. The times are simulated.
128 devices in a mesh: src: 8 (over z, core), tgt: 16 (over x, y).
Axes of the slice: x: 4, y: 4, z: 4, core: 2. Of those that a mesh axis runs over, the one named last changes fastest.
Arguments:
- src_emb: bfloat16 [32768, 1024], P(('src', 'tgt')), may hold values from 0 to 500, as said below
- tgt_emb: bfloat16 [8192, 1024], P('tgt'), may hold values from 0 to 500, as said below
- pair_list: int32 [128, 8], P('src'), may hold values from 0 to 31, as said below
- fwd_idx: int32 [32768, 16], P('src'), may hold values from 0 to 8191, as said below
- bwd_idx: int32 [8192, 16], P('tgt'), may hold values from 0 to 32767, as said below
Outputs:
- src_best: float32 [32768], P(('src', 'tgt'))
- tgt_best: float32 [8192], P('tgt')
Inputs may be any that keep to these rules, and one draw needn't show every extreme that they name: src_emb entries are positive. tgt_emb entries are positive. `pair_list`: each row names 8 distinct target blocks in ascending order. Row b names block c whenever c mod 128 equals b, so every target block is named. All 2 blocks of one tgt index, the same for every row, are named in every row. `fwd_idx`: entry [i, k] is a target row of a block named in row i // 256 of pair_list; entries may repeat. `bwd_idx`: entry [j, k] is a source row of a block whose pair_list row names block j // 256; entries may repeat.
All inputs are finite; a program needn't handle non-finite values.
Results may differ from a plain program's by a relative error of at most 0.00091.
Values may be sent and summed in bfloat16 or wider, within the bound.
A program may use at most 64 MiB of HBM per device.

v0:
```python
import jax
import jax.numpy as jnp
from jax import lax
from jax.sharding import PartitionSpec as P

BLOCK = 256
TB_DEV = 2


def unit_rows(values):
    wide = values.astype(jnp.float32)
    factor = lax.rsqrt(jnp.sum(wide * wide, axis=1, keepdims=True) + 1e-06)
    return (wide * factor).astype(jnp.bfloat16)


def body(src_emb, tgt_emb, pair_list, fwd_idx, bwd_idx):
    src_pos = lax.axis_index("src")
    tgt_pos = lax.axis_index("tgt")
    src_unit = unit_rows(src_emb)
    tgt_unit = unit_rows(tgt_emb)
    neighbours = fwd_idx.shape[1]
    src_rows_dev = src_unit.shape[0]
    tgt_rows_dev = tgt_unit.shape[0]
    tgt_first = tgt_pos * TB_DEV
    group_unit = lax.all_gather(src_unit, "tgt", axis=0, tiled=True)
    group_blocks = pair_list.shape[0]
    group_first = src_pos * group_blocks
    own_ids = tgt_first + jnp.arange(TB_DEV, dtype=jnp.int32)
    listed_mask = jnp.any(pair_list[:, :, None] == own_ids[None, None, :], axis=1)
    column_mask = jnp.repeat(listed_mask, BLOCK, axis=1)
    block_active = jnp.any(listed_mask, axis=1)
    column_base = tgt_first * BLOCK

    def similar(block_id):
        rows = lax.dynamic_slice_in_dim(group_unit, block_id * BLOCK, BLOCK, 0)
        return jnp.einsum("id,jd->ij", rows, tgt_unit, preferred_element_type=jnp.float32)

    def neighbour_terms(block_id):
        scores = similar(block_id)
        fwd_near = lax.dynamic_slice_in_dim(fwd_idx, block_id * BLOCK, BLOCK, 0) - column_base
        fwd_hit = (fwd_near >= 0) & (fwd_near < tgt_rows_dev)
        fwd_value = jnp.take_along_axis(scores, jnp.clip(fwd_near, 0, tgt_rows_dev - 1), axis=1)
        fwd_row = jnp.sum(jnp.where(fwd_hit, fwd_value, 0.0), axis=1)
        bwd_hit = bwd_idx // BLOCK == group_first + block_id
        bwd_value = jnp.take_along_axis(scores.T, bwd_idx % BLOCK, axis=1)
        bwd_row = jnp.sum(jnp.where(bwd_hit, bwd_value, 0.0), axis=1)
        return (scores, fwd_row, bwd_row)

    def skipped(block_id):
        return (
            jnp.zeros((BLOCK, tgt_rows_dev), jnp.float32),
            jnp.zeros((BLOCK,), jnp.float32),
            jnp.zeros((tgt_rows_dev,), jnp.float32),
        )

    def first_pass(block_id, carry):
        fwd_part, bwd_part, stored = carry
        scores, fwd_row, bwd_row = lax.cond(
            block_active[block_id], neighbour_terms, skipped, block_id
        )
        fwd_part = lax.dynamic_update_slice_in_dim(fwd_part, fwd_row[None, :], block_id, 0)
        bwd_part = bwd_part + bwd_row
        return (fwd_part, bwd_part, stored)

    stored_init = jnp.zeros((1, 1, 1), jnp.float32)
    fwd_part, bwd_part, stored = lax.fori_loop(
        0,
        group_blocks,
        first_pass,
        (
            jnp.zeros((group_blocks, BLOCK), jnp.float32),
            jnp.zeros((tgt_rows_dev,), jnp.float32),
            stored_init,
        ),
    )
    fwd_mean = lax.psum(fwd_part.reshape(-1), "tgt").reshape(group_blocks, BLOCK) / neighbours
    bwd_mean = lax.psum(bwd_part, "src") / neighbours

    def margin_rows(args):
        block_id, scores = args
        fwd_rows = lax.dynamic_index_in_dim(fwd_mean, block_id, 0, keepdims=False)
        ratio = 2.0 * scores / (fwd_rows[:, None] + bwd_mean[None, :])
        return jnp.where(column_mask[block_id][None, :], ratio, 0.0)

    def active_margins(block_id):
        return margin_rows((block_id, similar(block_id)))

    def second_pass(block_id, carry):
        src_peak, tgt_peak = carry
        ratio = lax.cond(
            block_active[block_id],
            lambda b: active_margins(b),
            lambda b: jnp.zeros((BLOCK, tgt_rows_dev), jnp.float32),
            block_id,
        )
        src_peak = lax.dynamic_update_slice_in_dim(
            src_peak, jnp.max(ratio, axis=1)[None, :], block_id, 0
        )
        tgt_peak = jnp.maximum(tgt_peak, jnp.max(ratio, axis=0))
        return (src_peak, tgt_peak)

    src_peak, tgt_peak = lax.fori_loop(
        0,
        group_blocks,
        second_pass,
        (jnp.zeros((group_blocks, BLOCK), jnp.float32), jnp.zeros((tgt_rows_dev,), jnp.float32)),
    )
    group_best = lax.pmax(src_peak.reshape(-1), "tgt")
    src_best = lax.dynamic_slice_in_dim(group_best, tgt_pos * src_rows_dev, src_rows_dev, 0)
    tgt_best = lax.pmax(tgt_peak, "src")
    return (src_best, tgt_best)


def solution(mesh):
    return jax.shard_map(
        body,
        mesh=mesh,
        in_specs=(
            P(("src", "tgt"), None),
            P("tgt", None),
            P("src", None),
            P("src", None),
            P("tgt", None),
        ),
        out_specs=(P(("src", "tgt")), P("tgt")),
        check_vma=False,
    )
```

profile of v0, /device:TPU:1, one launch (start us, length us, event | category | flops | bytes accessed | tf_op | source)
XLA Modules:
  0.0 1977.1 jit_solution(5233314779979377362)
XLA Ops:
  14.2 70.3 %all-gather.2.cloned.1.call-done = bf16[4096,1024]{1,0:T(8,128)(2,1)} async-done(((bf16[256,1024]{1,0:T(8,128)(2,1)}), bf16[4096,1024]{1,0:T(8,128)(2,1)}) %all-gather.2.cloned.1.call-update) | async-done | bytes 8388624 | tf_op jit(solution)/shard_map/all_gather | solution.py:25
  84.5 1670.2 %while.32 = (s32[]{:T(128)}, f32[16,256]{1,0:T(8,128)S(1)}, f32[512]{0:T(512)S(1)}, pred[16]{0:T(512)(128)(4,1)S(1)}, s32[512,16]{1,0:T(8,128)S(1)}, /*index=5*/...) while((s32[]{:T(128)}, f32[16,256]{1,0:T(8,128)S(1)}, ...), condition=%wide.region_8.9_spmd.clone, body=%wide.region_3.8_spmd.clone.sunk | while | flops 268927232 | bytes 2698536 | solution.py:66
  85.8 103.0 %conditional.6 = (f32[512]{0:T(512)S(1)}, f32[1,256]{1,0:T(1,128)S(1)}) conditional(s32[]{:T(128)} %bitcast.24, () %tuple.99, (s32[512,16]{1,0:T(8,128)S(1)}, s32[]{:T(128)}, s32[]{:T(128)}, bf16[4096,1024]{1,0:T(8,128)(2,1)}, bf16[512,1024]{1,0:T(8,128)(2,1)S(1)}, /*index=5*/s32[4096,16]{1,0:T(8,128)}, s32[]{:T(128)}) %tuple.100), branch_computations={%region_4.4_spmd, %region_5.7_spmd} | conditional | flops 268926208 | bytes 2690146 | solution.py:58
  122.8 65.5 %gather_fusion = f32[8192]{0:T(1024)S(1)} fusion(f32[512,256]{0,1:T(8,128)S(1)} %bitcast.26, s32[8192]{0:T(1024)S(1)} %reshape.63), kind=kCustom, calls=%fused_computation | custom fusion | bytes 131072 | tf_op jit(solution)/shard_map/while/body/eval_jaxpr/cond/branch_1_fun/jit(take_along_axis)/gather | solution.py:45
  190.2 103.0 %conditional.6 = (f32[512]{0:T(512)S(1)}, f32[1,256]{1,0:T(1,128)S(1)}) conditional(s32[]{:T(128)} %bitcast.24, () %tuple.99, (s32[512,16]{1,0:T(8,128)S(1)}, s32[]{:T(128)}, s32[]{:T(128)}, bf16[4096,1024]{1,0:T(8,128)(2,1)}, bf16[512,1024]{1,0:T(8,128)(2,1)S(1)}, /*index=5*/s32[4096,16]{1,0:T(8,128)}, s32[]{:T(128)}) %tuple.100), branch_computations={%region_4.4_spmd, %region_5.7_spmd} | conditional | flops 268926208 | bytes 2690146 | solution.py:58
  227.1 65.5 %gather_fusion = f32[8192]{0:T(1024)S(1)} fusion(f32[512,256]{0,1:T(8,128)S(1)} %bitcast.26, s32[8192]{0:T(1024)S(1)} %reshape.63), kind=kCustom, calls=%fused_computation | custom fusion | bytes 131072 | tf_op jit(solution)/shard_map/while/body/eval_jaxpr/cond/branch_1_fun/jit(take_along_axis)/gather | solution.py:45
  294.6 103.0 %conditional.6 = (f32[512]{0:T(512)S(1)}, f32[1,256]{1,0:T(1,128)S(1)}) conditional(s32[]{:T(128)} %bitcast.24, () %tuple.99, (s32[512,16]{1,0:T(8,128)S(1)}, s32[]{:T(128)}, s32[]{:T(128)}, bf16[4096,1024]{1,0:T(8,128)(2,1)}, bf16[512,1024]{1,0:T(8,128)(2,1)S(1)}, /*index=5*/s32[4096,16]{1,0:T(8,128)}, s32[]{:T(128)}) %tuple.100), branch_computations={%region_4.4_spmd, %region_5.7_spmd} | conditional | flops 268926208 | bytes 2690146 | solution.py:58
  331.5 65.5 %gather_fusion = f32[8192]{0:T(1024)S(1)} fusion(f32[512,256]{0,1:T(8,128)S(1)} %bitcast.26, s32[8192]{0:T(1024)S(1)} %reshape.63), kind=kCustom, calls=%fused_computation | custom fusion | bytes 131072 | tf_op jit(solution)/shard_map/while/body/eval_jaxpr/cond/branch_1_fun/jit(take_along_axis)/gather | solution.py:45
  399.0 103.0 %conditional.6 = (f32[512]{0:T(512)S(1)}, f32[1,256]{1,0:T(1,128)S(1)}) conditional(s32[]{:T(128)} %bitcast.24, () %tuple.99, (s32[512,16]{1,0:T(8,128)S(1)}, s32[]{:T(128)}, s32[]{:T(128)}, bf16[4096,1024]{1,0:T(8,128)(2,1)}, bf16[512,1024]{1,0:T(8,128)(2,1)S(1)}, /*index=5*/s32[4096,16]{1,0:T(8,128)}, s32[]{:T(128)}) %tuple.100), branch_computations={%region_4.4_spmd, %region_5.7_spmd} | conditional | flops 268926208 | bytes 2690146 | solution.py:58
  435.9 65.5 %gather_fusion = f32[8192]{0:T(1024)S(1)} fusion(f32[512,256]{0,1:T(8,128)S(1)} %bitcast.26, s32[8192]{0:T(1024)S(1)} %reshape.63), kind=kCustom, calls=%fused_computation | custom fusion | bytes 131072 | tf_op jit(solution)/shard_map/while/body/eval_jaxpr/cond/branch_1_fun/jit(take_along_axis)/gather | solution.py:45
  503.4 103.0 %conditional.6 = (f32[512]{0:T(512)S(1)}, f32[1,256]{1,0:T(1,128)S(1)}) conditional(s32[]{:T(128)} %bitcast.24, () %tuple.99, (s32[512,16]{1,0:T(8,128)S(1)}, s32[]{:T(128)}, s32[]{:T(128)}, bf16[4096,1024]{1,0:T(8,128)(2,1)}, bf16[512,1024]{1,0:T(8,128)(2,1)S(1)}, /*index=5*/s32[4096,16]{1,0:T(8,128)}, s32[]{:T(128)}) %tuple.100), branch_computations={%region_4.4_spmd, %region_5.7_spmd} | conditional | flops 268926208 | bytes 2690146 | solution.py:58
  540.3 65.5 %gather_fusion = f32[8192]{0:T(1024)S(1)} fusion(f32[512,256]{0,1:T(8,128)S(1)} %bitcast.26, s32[8192]{0:T(1024)S(1)} %reshape.63), kind=kCustom, calls=%fused_computation | custom fusion | bytes 131072 | tf_op jit(solution)/shard_map/while/body/eval_jaxpr/cond/branch_1_fun/jit(take_along_axis)/gather | solution.py:45
  607.8 103.0 %conditional.6 = (f32[512]{0:T(512)S(1)}, f32[1,256]{1,0:T(1,128)S(1)}) conditional(s32[]{:T(128)} %bitcast.24, () %tuple.99, (s32[512,16]{1,0:T(8,128)S(1)}, s32[]{:T(128)}, s32[]{:T(128)}, bf16[4096,1024]{1,0:T(8,128)(2,1)}, bf16[512,1024]{1,0:T(8,128)(2,1)S(1)}, /*index=5*/s32[4096,16]{1,0:T(8,128)}, s32[]{:T(128)}) %tuple.100), branch_computations={%region_4.4_spmd, %region_5.7_spmd} | conditional | flops 268926208 | bytes 2690146 | solution.py:58
  644.7 65.5 %gather_fusion = f32[8192]{0:T(1024)S(1)} fusion(f32[512,256]{0,1:T(8,128)S(1)} %bitcast.26, s32[8192]{0:T(1024)S(1)} %reshape.63), kind=kCustom, calls=%fused_computation | custom fusion | bytes 131072 | tf_op jit(solution)/shard_map/while/body/eval_jaxpr/cond/branch_1_fun/jit(take_along_axis)/gather | solution.py:45
  712.2 103.0 %conditional.6 = (f32[512]{0:T(512)S(1)}, f32[1,256]{1,0:T(1,128)S(1)}) conditional(s32[]{:T(128)} %bitcast.24, () %tuple.99, (s32[512,16]{1,0:T(8,128)S(1)}, s32[]{:T(128)}, s32[]{:T(128)}, bf16[4096,1024]{1,0:T(8,128)(2,1)}, bf16[512,1024]{1,0:T(8,128)(2,1)S(1)}, /*index=5*/s32[4096,16]{1,0:T(8,128)}, s32[]{:T(128)}) %tuple.100), branch_computations={%region_4.4_spmd, %region_5.7_spmd} | conditional | flops 268926208 | bytes 2690146 | solution.py:58
  749.1 65.5 %gather_fusion = f32[8192]{0:T(1024)S(1)} fusion(f32[512,256]{0,1:T(8,128)S(1)} %bitcast.26, s32[8192]{0:T(1024)S(1)} %reshape.63), kind=kCustom, calls=%fused_computation | custom fusion | bytes 131072 | tf_op jit(solution)/shard_map/while/body/eval_jaxpr/cond/branch_1_fun/jit(take_along_axis)/gather | solution.py:45
  816.6 103.0 %conditional.6 = (f32[512]{0:T(512)S(1)}, f32[1,256]{1,0:T(1,128)S(1)}) conditional(s32[]{:T(128)} %bitcast.24, () %tuple.99, (s32[512,16]{1,0:T(8,128)S(1)}, s32[]{:T(128)}, s32[]{:T(128)}, bf16[4096,1024]{1,0:T(8,128)(2,1)}, bf16[512,1024]{1,0:T(8,128)(2,1)S(1)}, /*index=5*/s32[4096,16]{1,0:T(8,128)}, s32[]{:T(128)}) %tuple.100), branch_computations={%region_4.4_spmd, %region_5.7_spmd} | conditional | flops 268926208 | bytes 2690146 | solution.py:58
  853.5 65.5 %gather_fusion = f32[8192]{0:T(1024)S(1)} fusion(f32[512,256]{0,1:T(8,128)S(1)} %bitcast.26, s32[8192]{0:T(1024)S(1)} %reshape.63), kind=kCustom, calls=%fused_computation | custom fusion | bytes 131072 | tf_op jit(solution)/shard_map/while/body/eval_jaxpr/cond/branch_1_fun/jit(take_along_axis)/gather | solution.py:45
  921.0 103.0 %conditional.6 = (f32[512]{0:T(512)S(1)}, f32[1,256]{1,0:T(1,128)S(1)}) conditional(s32[]{:T(128)} %bitcast.24, () %tuple.99, (s32[512,16]{1,0:T(8,128)S(1)}, s32[]{:T(128)}, s32[]{:T(128)}, bf16[4096,1024]{1,0:T(8,128)(2,1)}, bf16[512,1024]{1,0:T(8,128)(2,1)S(1)}, /*index=5*/s32[4096,16]{1,0:T(8,128)}, s32[]{:T(128)}) %tuple.100), branch_computations={%region_4.4_spmd, %region_5.7_spmd} | conditional | flops 268926208 | bytes 2690146 | solution.py:58
  957.9 65.5 %gather_fusion = f32[8192]{0:T(1024)S(1)} fusion(f32[512,256]{0,1:T(8,128)S(1)} %bitcast.26, s32[8192]{0:T(1024)S(1)} %reshape.63), kind=kCustom, calls=%fused_computation | custom fusion | bytes 131072 | tf_op jit(solution)/shard_map/while/body/eval_jaxpr/cond/branch_1_fun/jit(take_along_axis)/gather | solution.py:45
  1025.4 103.0 %conditional.6 = (f32[512]{0:T(512)S(1)}, f32[1,256]{1,0:T(1,128)S(1)}) conditional(s32[]{:T(128)} %bitcast.24, () %tuple.99, (s32[512,16]{1,0:T(8,128)S(1)}, s32[]{:T(128)}, s32[]{:T(128)}, bf16[4096,1024]{1,0:T(8,128)(2,1)}, bf16[512,1024]{1,0:T(8,128)(2,1)S(1)}, /*index=5*/s32[4096,16]{1,0:T(8,128)}, s32[]{:T(128)}) %tuple.100), branch_computations={%region_4.4_spmd, %region_5.7_spmd} | conditional | flops 268926208 | bytes 2690146 | solution.py:58
  1062.3 65.5 %gather_fusion = f32[8192]{0:T(1024)S(1)} fusion(f32[512,256]{0,1:T(8,128)S(1)} %bitcast.26, s32[8192]{0:T(1024)S(1)} %reshape.63), kind=kCustom, calls=%fused_computation | custom fusion | bytes 131072 | tf_op jit(solution)/shard_map/while/body/eval_jaxpr/cond/branch_1_fun/jit(take_along_axis)/gather | solution.py:45
  1129.7 103.0 %conditional.6 = (f32[512]{0:T(512)S(1)}, f32[1,256]{1,0:T(1,128)S(1)}) conditional(s32[]{:T(128)} %bitcast.24, () %tuple.99, (s32[512,16]{1,0:T(8,128)S(1)}, s32[]{:T(128)}, s32[]{:T(128)}, bf16[4096,1024]{1,0:T(8,128)(2,1)}, bf16[512,1024]{1,0:T(8,128)(2,1)S(1)}, /*index=5*/s32[4096,16]{1,0:T(8,128)}, s32[]{:T(128)}) %tuple.100), branch_computations={%region_4.4_spmd, %region_5.7_spmd} | conditional | flops 268926208 | bytes 2690146 | solution.py:58
  1166.7 65.5 %gather_fusion = f32[8192]{0:T(1024)S(1)} fusion(f32[512,256]{0,1:T(8,128)S(1)} %bitcast.26, s32[8192]{0:T(1024)S(1)} %reshape.63), kind=kCustom, calls=%fused_computation | custom fusion | bytes 131072 | tf_op jit(solution)/shard_map/while/body/eval_jaxpr/cond/branch_1_fun/jit(take_along_axis)/gather | solution.py:45
  1234.1 103.0 %conditional.6 = (f32[512]{0:T(512)S(1)}, f32[1,256]{1,0:T(1,128)S(1)}) conditional(s32[]{:T(128)} %bitcast.24, () %tuple.99, (s32[512,16]{1,0:T(8,128)S(1)}, s32[]{:T(128)}, s32[]{:T(128)}, bf16[4096,1024]{1,0:T(8,128)(2,1)}, bf16[512,1024]{1,0:T(8,128)(2,1)S(1)}, /*index=5*/s32[4096,16]{1,0:T(8,128)}, s32[]{:T(128)}) %tuple.100), branch_computations={%region_4.4_spmd, %region_5.7_spmd} | conditional | flops 268926208 | bytes 2690146 | solution.py:58
  1271.0 65.5 %gather_fusion = f32[8192]{0:T(1024)S(1)} fusion(f32[512,256]{0,1:T(8,128)S(1)} %bitcast.26, s32[8192]{0:T(1024)S(1)} %reshape.63), kind=kCustom, calls=%fused_computation | custom fusion | bytes 131072 | tf_op jit(solution)/shard_map/while/body/eval_jaxpr/cond/branch_1_fun/jit(take_along_axis)/gather | solution.py:45
  1338.5 103.0 %conditional.6 = (f32[512]{0:T(512)S(1)}, f32[1,256]{1,0:T(1,128)S(1)}) conditional(s32[]{:T(128)} %bitcast.24, () %tuple.99, (s32[512,16]{1,0:T(8,128)S(1)}, s32[]{:T(128)}, s32[]{:T(128)}, bf16[4096,1024]{1,0:T(8,128)(2,1)}, bf16[512,1024]{1,0:T(8,128)(2,1)S(1)}, /*index=5*/s32[4096,16]{1,0:T(8,128)}, s32[]{:T(128)}) %tuple.100), branch_computations={%region_4.4_spmd, %region_5.7_spmd} | conditional | flops 268926208 | bytes 2690146 | solution.py:58
  1375.4 65.5 %gather_fusion = f32[8192]{0:T(1024)S(1)} fusion(f32[512,256]{0,1:T(8,128)S(1)} %bitcast.26, s32[8192]{0:T(1024)S(1)} %reshape.63), kind=kCustom, calls=%fused_computation | custom fusion | bytes 131072 | tf_op jit(solution)/shard_map/while/body/eval_jaxpr/cond/branch_1_fun/jit(take_along_axis)/gather | solution.py:45
  1442.9 103.0 %conditional.6 = (f32[512]{0:T(512)S(1)}, f32[1,256]{1,0:T(1,128)S(1)}) conditional(s32[]{:T(128)} %bitcast.24, () %tuple.99, (s32[512,16]{1,0:T(8,128)S(1)}, s32[]{:T(128)}, s32[]{:T(128)}, bf16[4096,1024]{1,0:T(8,128)(2,1)}, bf16[512,1024]{1,0:T(8,128)(2,1)S(1)}, /*index=5*/s32[4096,16]{1,0:T(8,128)}, s32[]{:T(128)}) %tuple.100), branch_computations={%region_4.4_spmd, %region_5.7_spmd} | conditional | flops 268926208 | bytes 2690146 | solution.py:58
  1479.8 65.5 %gather_fusion = f32[8192]{0:T(1024)S(1)} fusion(f32[512,256]{0,1:T(8,128)S(1)} %bitcast.26, s32[8192]{0:T(1024)S(1)} %reshape.63), kind=kCustom, calls=%fused_computation | custom fusion | bytes 131072 | tf_op jit(solution)/shard_map/while/body/eval_jaxpr/cond/branch_1_fun/jit(take_along_axis)/gather | solution.py:45
  1547.3 103.0 %conditional.6 = (f32[512]{0:T(512)S(1)}, f32[1,256]{1,0:T(1,128)S(1)}) conditional(s32[]{:T(128)} %bitcast.24, () %tuple.99, (s32[512,16]{1,0:T(8,128)S(1)}, s32[]{:T(128)}, s32[]{:T(128)}, bf16[4096,1024]{1,0:T(8,128)(2,1)}, bf16[512,1024]{1,0:T(8,128)(2,1)S(1)}, /*index=5*/s32[4096,16]{1,0:T(8,128)}, s32[]{:T(128)}) %tuple.100), branch_computations={%region_4.4_spmd, %region_5.7_spmd} | conditional | flops 268926208 | bytes 2690146 | solution.py:58
  1651.7 103.0 %conditional.6 = (f32[512]{0:T(512)S(1)}, f32[1,256]{1,0:T(1,128)S(1)}) conditional(s32[]{:T(128)} %bitcast.24, () %tuple.99, (s32[512,16]{1,0:T(8,128)S(1)}, s32[]{:T(128)}, s32[]{:T(128)}, bf16[4096,1024]{1,0:T(8,128)(2,1)}, bf16[512,1024]{1,0:T(8,128)(2,1)S(1)}, /*index=5*/s32[4096,16]{1,0:T(8,128)}, s32[]{:T(128)}) %tuple.100), branch_computations={%region_4.4_spmd, %region_5.7_spmd} | conditional | flops 268926208 | bytes 2690146 | solution.py:58
  (394 shorter events, 1029.4 us)
Async XLA Ops:
  7.2 3.5 copy-start.1
  7.2 77.3 %all-gather.2.cloned.1.call-start = ((), (), s32[]{:S(2)}) async-start(), calls=%async_computation | async-start | bytes 8912896 | tf_op jit(solution)/shard_map/all_gather | solution.py:25
  8.5 4.2 copy-start.4
  8.5 4.3 copy-start.5
  8.5 5.1 copy-start
  84.5 1752.5 %copy-start.2 = (pred[16,2]{1,0:T(8,128)(4,1)S(1)}, pred[16,2]{1,0:T(8,128)(4,1)}, u32[]{:S(2)}) copy-start(pred[16,2]{1,0:T(8,128)(4,1)} %copy.13) | copy-start | bytes 100
  84.5 1752.5 %copy-start.3 = (f32[512]{0:T(512)S(1)}, f32[512]{0:T(512)}, u32[]{:S(2)}) copy-start(f32[512]{0:T(512)} %custom-call.5) | copy-start | bytes 6148
Sparse Core Ops, SparseCore 0:
  10.8 73.6 all-gather.1
where the time goes:
time: 1970 us; the launch traced here: 1980 us
  local copies, waits for them, and re-layouts  1610 us (82%)
  blocking collectives  165 us (8%)
  waiting for transfers between devices  70.4 us (4%)
  matrix products  50.3 us (3%)
  other arithmetic  46.4 us (2%)
  loops' own time  24.6 us (1%)
    gather x48, local copies, waits for them, and re-layouts, neighbour_terms(): bwd_value = jnp.take_along_axis(scores.T, bwd_idx % BLOCK, axis=1)  1050 us
    gather x48, local copies, waits for them, and re-layouts, neighbour_terms(): jnp.take_along_axis(scores, jnp.clip(fwd_near, 0, tgt_rows_dev - 1), axis=1)  527 us
    all_gather x1, waiting for transfers between devices, body(): group_unit = lax.all_gather(src_unit, 'tgt', axis=0, tiled=True)  70.3 us
    pmax x1, blocking collectives, body(): group_best = lax.pmax(src_peak.reshape(-1), 'tgt')  56.2 us
    psum x1, blocking collectives, body(): lax.psum(fwd_part.reshape(-1), 'tgt').reshape(group_blocks, BLOCK)  55.6 us
    dot_general x32, matrix products, similar(): jnp.einsum('id,jd->ij', rows, tgt_unit, preferred_element_type=jnp.float32)  50.3 us
  transfers between devices with their start and end apart: 1, of which 1 were waited for; matrix products, arithmetic and copies ran while one was open for 0% of the time, Pallas kernels for 0%

commit v1 on v0

v1 whole, which is shorter than its diff:
```python
import jax
import jax.numpy as jnp
from jax import lax
from jax.experimental import pallas as pl
from jax.experimental.pallas import tpu as pltpu
from jax.sharding import PartitionSpec as P

D = 1024
MESH = pl.DeviceIdType.MESH
F32 = jnp.float32
BF16 = jnp.bfloat16
I32 = jnp.int32

ROW_REL = (0, 0, 3, 1, 3, 1, 2, 2)
COL_SLOT = ((0, 0), (0, 0), (0, 1), (0, 1), (3, 0), (1, 0), (3, 1), (1, 1),
            (3, 0), (1, 0), (3, 1), (1, 1), (2, 0), (2, 1), (2, 0), (2, 1))


def aligned(value, step):
    return pl.multiple_of(value, step)


def kernel(src_hbm, tgt_hbm, pair_ref, fwd_hbm, bwd_hbm, src_out, tgt_out,
           src_raw, tgt_raw, src_buf, tgt_buf, scores, fwd_raw, bwd_raw, fwd_pos, bwd_pos,
           fwd_val, bwd_val, weight, frow, fcol, brow, fwd_part, fwd_in, bwd_part, bwd_zin,
           bwd_two, bwd_xin, src_part, src_in, tgt_part, tgt_xin, tgt_two, tgt_zin,
           load_sem, send_sem, recv_sem):
    s = lax.axis_index("src")
    t = lax.axis_index("tgt")
    core = lax.rem(s, 2)
    z = s // 2
    x = t // 4
    y = lax.rem(t, 4)

    def y_dev(d):
        return (s, 4 * x + lax.rem(y + d, 4))

    def x_dev(d):
        return (s, 4 * lax.rem(x + d, 4) + y)

    def zc_dev(d):
        dz, dc = d // 2, d % 2
        return (2 * lax.rem(z + dz, 4) + lax.rem(core + dc, 2), t)

    src_load = pltpu.make_async_copy(src_hbm, src_raw, load_sem.at[0])
    src_load.start()
    tgt_load = pltpu.make_async_copy(tgt_hbm, tgt_raw, load_sem.at[1])
    tgt_load.start()
    bwd_load = pltpu.make_async_copy(bwd_hbm, bwd_raw.at[0], load_sem.at[2])
    bwd_load.start()
    fwd_load = pltpu.make_async_copy(
        fwd_hbm.at[:, pl.ds(aligned(x * 1024, 1024), 1024)], fwd_raw, load_sem.at[3])
    fwd_load.start()

    barrier = pltpu.get_barrier_semaphore()
    for d in (1, 2, 3):
        pl.semaphore_signal(barrier, inc=1, device_id=y_dev(d), device_id_type=MESH)
        pl.semaphore_signal(barrier, inc=1, device_id=x_dev(d), device_id_type=MESH)
    for d in range(1, 8):
        pl.semaphore_signal(barrier, inc=1, device_id=zc_dev(d), device_id_type=MESH)

    def remote(src, dst, sem, device):
        return pltpu.make_async_remote_copy(
            src_ref=src, dst_ref=dst, send_sem=send_sem.at[sem], recv_sem=recv_sem.at[sem],
            device_id=device, device_id_type=MESH)

    def normalise(raw, buf, raw_first, buf_first, count):
        def step(i, _):
            wide = raw[pl.ds(aligned(raw_first + i * 16, 16), 16), :].astype(F32)
            factor = lax.rsqrt(jnp.sum(wide * wide, axis=1, keepdims=True) + 1e-06)
            buf[pl.ds(aligned(buf_first + i * 16, 16), 16), :] = (wide * factor).astype(BF16)
            return 0
        lax.fori_loop(0, count // 16, step, 0, unroll=4)

    c256 = core * 256
    c128 = core * 128
    src_load.wait()
    normalise(src_raw, src_buf, 0, 0, 256)
    tgt_load.wait()
    normalise(tgt_raw, tgt_buf, c256, c256, 256)
    pl.semaphore_wait(barrier, 13)

    def srow(first, count):
        return src_buf.at[pl.ds(first, count), :]

    def trow(first, count, step=64):
        return tgt_buf.at[pl.ds(aligned(first, step), count), :]

    own_copies = (
        remote(srow(0, 128), srow(256, 128), 0, y_dev(1)),
        remote(srow(128, 128), srow(384, 128), 1, y_dev(3)),
        remote(trow(c256, 128), trow(512 + c256, 128), 2, x_dev(1)),
        remote(trow(c256 + 128, 128), trow(640 + c256, 128), 3, x_dev(3)),
        remote(srow(128, 128), srow(512, 128), 4, y_dev(1)),
        remote(srow(0, 128), srow(640, 128), 5, y_dev(3)),
        remote(trow(c256 + 128, 128), trow(1024 + c256, 128), 6, x_dev(1)),
        remote(trow(c256, 128), trow(1152 + c256, 128), 7, x_dev(3)),
    )
    idx_copies = (
        remote(bwd_hbm, bwd_raw.at[3], 8, x_dev(1)),
        remote(bwd_hbm, bwd_raw.at[1], 9, x_dev(3)),
        remote(bwd_hbm, bwd_raw.at[2], 10, x_dev(2)),
    )
    for copy in own_copies[:4]:
        copy.start()
    for copy in idx_copies:
        copy.start()
    for copy in own_copies[4:]:
        copy.start()

    normalise(tgt_raw, tgt_buf, 256 - c256, 256 - c256, 256)

    def weight_row(rel, _):
        row = 4 * x + lax.rem(y + rel, 4)
        names = [pair_ref[k, row] for k in range(8)]
        for relx in range(4):
            for p in range(2):
                block = 2 * (4 * lax.rem(x + relx, 4) + y) + p
                hit = jnp.int32(0)
                for k in range(8):
                    hit = hit + jnp.where(names[k] == block, 1, 0)
                value = jnp.full((1, 128), jnp.where(hit > 0, 2.0, 0.0), F32)
                for chunk in range(16):
                    if COL_SLOT[chunk] == (relx, p):
                        weight[rel, :, chunk * 128:(chunk + 1) * 128] = value
        return 0

    lax.fori_loop(0, 4, weight_row, 0)

    lane = lax.broadcasted_iota(I32, (16, 128), 1)

    def far(first, second):
        return jnp.where(lane < 64, first, second), jnp.where(lane < 64, second, first)

    fwd_load.wait()
    fwd_pos[...] = jnp.full((1024, 128), -1, I32)

    def fwd_half(rel, half):
        return fwd_raw[:, pl.ds(aligned(lax.rem(y + rel, 4) * 256 + half * 128, 128), 128)]

    f6, f7 = far(fwd_half(2, 0), fwd_half(2, 1))
    fwd_chunks = (fwd_half(0, 0), fwd_half(0, 1), fwd_half(3, 0), fwd_half(1, 1),
                  fwd_half(3, 1), fwd_half(1, 0), f6, f7)
    for chunk, index in enumerate(fwd_chunks):
        block = index >> 8
        inner = index & 255
        p = block & 1
        rel = ((block >> 3) - x) & 3
        upper = inner >= 128
        near = jnp.where(upper == (rel == 1), 512, jnp.where(rel == 1, 1152, 896))
        quarter = inner >> 6
        distant = jnp.where(quarter == 0, 1536, jnp.where(quarter == 3, 1408,
                            jnp.where(quarter == 2, 1664, 1792))) - p * 128
        base = jnp.where(rel == 0, 0, jnp.where(rel == 2, distant, near))
        column = jnp.where(((block >> 1) & 3) == y, base + p * 256 + inner, -1)
        fwd_pos[chunk * 128:(chunk + 1) * 128, 0:16] = jnp.transpose(column)

    def bwd_rows(index):
        block = index >> 8
        inner = index & 255
        rel = ((block & 3) - y) & 3
        upper = inner >= 128
        near = jnp.where(upper == (rel == 1), 256, jnp.where(rel == 1, 640, 384))
        quarter = inner >> 6
        distant = jnp.where(quarter == 0, 768, jnp.where(quarter == 3, 640,
                            jnp.where(quarter == 2, 768, 896)))
        base = jnp.where(rel == 0, 0, jnp.where(rel == 2, distant, near))
        hit = (block >> 2) == s * 4 + x
        return jnp.where(hit, base + inner, -1)

    def bwd_put(chunk, index):
        bwd_pos[:, chunk * 128:(chunk + 1) * 128] = bwd_rows(index)

    def bwd_half(rel, p, half):
        first = p * 256 + half * 128
        return bwd_raw[rel, :, first:first + 128]

    bwd_load.wait()
    for chunk in range(4):
        bwd_put(chunk, bwd_half(0, chunk // 2, chunk % 2))

    fwd_val[...] = jnp.zeros((1024, 128), F32)
    bwd_val[...] = jnp.zeros((16, 2048), F32)

    def region(row, rows, col, cols):
        def dots(i, _):
            at = pl.ds(aligned(col + i * 256, 256), 256)
            scores[row:row + rows, at] = lax.dot_general(
                src_buf[row:row + rows, :], tgt_buf[at, :], (((1,), (1,)), ((), ())),
                preferred_element_type=F32)
            return 0
        lax.fori_loop(0, cols // 256, dots, 0)

        def fwd_rows(g, _):
            at = pl.ds(aligned(row + g * 8, 8), 8)
            index = fwd_pos[at, :]
            pick = index & 127
            where = index >> 7
            value = fwd_val[at, :]
            for chunk in range(col // 128, (col + cols) // 128):
                found = jnp.take_along_axis(
                    scores[at, chunk * 128:(chunk + 1) * 128], pick, axis=1,
                    mode="promise_in_bounds")
                value = jnp.where(where == chunk, found, value)
            fwd_val[at, :] = value
            return 0
        lax.fori_loop(0, rows // 8, fwd_rows, 0, unroll=4)

        def bwd_cols(i, _):
            at = pl.ds(aligned(col + i * 128, 128), 128)
            index0, index1 = bwd_pos[0:8, at], bwd_pos[8:16, at]
            pick0, pick1 = index0 & 7, index1 & 7
            where0, where1 = index0 >> 3, index1 >> 3

            def group(g, values):
                value0, value1 = values
                here = row // 8 + g
                part = scores[pl.ds(aligned(row + g * 8, 8), 8), at]
                found0 = jnp.take_along_axis(part, pick0, axis=0, mode="promise_in_bounds")
                found1 = jnp.take_along_axis(part, pick1, axis=0, mode="promise_in_bounds")
                return (jnp.where(where0 == here, found0, value0),
                        jnp.where(where1 == here, found1, value1))
            value0, value1 = lax.fori_loop(
                0, rows // 8, group, (bwd_val[0:8, at], bwd_val[8:16, at]), unroll=16)
            bwd_val[0:8, at] = value0
            bwd_val[8:16, at] = value1
            return 0
        lax.fori_loop(0, cols // 128, bwd_cols, 0)

    region(0, 256, 0, 512)

    for copy in own_copies[:4]:
        copy.wait_recv()
    far_copies = (
        remote(srow(256, 64), srow(768, 64), 11, y_dev(1)),
        remote(srow(448, 64), srow(832, 64), 12, y_dev(3)),
        remote(trow(512 + c256, 64), trow(1536 + c128, 64), 13, x_dev(1)),
        remote(trow(704 + c256, 64), trow(1600 + c128, 64), 14, x_dev(3)),
        remote(srow(320, 64), srow(960, 64), 15, y_dev(1)),
        remote(srow(384, 64), srow(896, 64), 16, y_dev(3)),
        remote(trow(576 + c256, 64), trow(1856 + c128, 64), 17, x_dev(1)),
        remote(trow(640 + c256, 64), trow(1792 + c128, 64), 18, x_dev(3)),
    )
    for copy in far_copies:
        copy.start()
    partner = zc_dev(1)
    pass_copies = (
        remote(trow(512 + c256, 256), trow(512 + c256, 256), 19, partner),
        remote(trow(1024 + c256, 256), trow(1024 + c256, 256), 20, partner),
        remote(trow(1536 + c128, 128), trow(1536 + c128, 128), 21, partner),
        remote(trow(1792 + c128, 128), trow(1792 + c128, 128), 22, partner),
    )
    pass_copies[0].start()
    for copy in idx_copies:
        copy.wait_recv()
    for p in range(2):
        bwd_put(4 + 2 * p, bwd_half(3, p, 0))
        bwd_put(5 + 2 * p, bwd_half(1, p, 1))
        bwd_put(8 + 2 * p, bwd_half(3, p, 1))
        bwd_put(9 + 2 * p, bwd_half(1, p, 0))
        near, distant = far(bwd_half(2, p, 0), bwd_half(2, p, 1))
        bwd_put(12 + p, near)
        bwd_put(14 + p, distant)
    pass_copies[0].wait_recv()
    region(0, 256, 512, 512)
    region(256, 256, 0, 1024)

    for copy in own_copies[4:]:
        copy.wait_recv()
    pass_copies[1].start()
    region(512, 256, 0, 1024)
    pass_copies[1].wait_recv()
    region(0, 768, 1024, 512)

    for copy in far_copies[:4]:
        copy.wait_recv()
    pass_copies[2].start()
    region(768, 128, 0, 1536)
    pass_copies[2].wait_recv()
    region(0, 896, 1536, 256)

    for copy in far_copies[4:]:
        copy.wait_recv()
    pass_copies[3].start()
    region(896, 128, 0, 1792)
    pass_copies[3].wait_recv()
    region(0, 1024, 1792, 256)

    lane1 = lane[0:1, :]

    def bwd_sum(chunk):
        return jnp.sum(bwd_val[:, chunk * 128:(chunk + 1) * 128], axis=0, keepdims=True)

    def unfar(first, second):
        return jnp.where(lane1 < 64, first, second), jnp.where(lane1 < 64, second, first)

    def natural_cols(get):
        blocks = [[None] * 4 for _ in range(4)]
        for chunk in range(4):
            blocks[0][chunk] = get(chunk)
        for p in range(2):
            blocks[3][2 * p] = get(4 + 2 * p)
            blocks[1][2 * p + 1] = get(5 + 2 * p)
            blocks[3][2 * p + 1] = get(8 + 2 * p)
            blocks[1][2 * p] = get(9 + 2 * p)
            blocks[2][2 * p], blocks[2][2 * p + 1] = unfar(get(12 + p), get(14 + p))
        return blocks

    def natural_rows(get):
        blocks = [[None] * 2 for _ in range(4)]
        blocks[0] = [get(0), get(1)]
        blocks[3] = [get(2), get(4)]
        blocks[1] = [get(5), get(3)]
        blocks[2] = list(unfar(get(6), get(7)))
        return blocks

    for rel, rows in enumerate(natural_cols(bwd_sum)):
        for i, value in enumerate(rows):
            bwd_part[lax.rem(x + rel, 4), i:i + 1, :] = value
    bwd_z = [remote(bwd_part, bwd_zin.at[d - 1], 22 + d, zc_dev(d)) for d in range(1, 8)]
    for copy in bwd_z:
        copy.start()

    def fwd_sum(chunk):
        values = jnp.transpose(fwd_val[chunk * 128:(chunk + 1) * 128, :])
        return jnp.sum(values[0:16, :], axis=0, keepdims=True)

    for rel, rows in enumerate(natural_rows(fwd_sum)):
        for i, value in enumerate(rows):
            fwd_part[lax.rem(y + rel, 4), i:i + 1, :] = value
    fwd_y = [remote(fwd_part, fwd_in.at[d - 1], 29 + d, y_dev(d)) for d in range(1, 4)]
    for copy in fwd_y:
        copy.start()

    for copy in bwd_z:
        copy.wait_recv()
    total = bwd_part[...]
    for d in range(7):
        total = total + bwd_zin[d]
    bwd_two[...] = total
    bwd_x = [remote(bwd_two, bwd_xin.at[d - 1], 32 + d, x_dev(d)) for d in range(1, 4)]
    for copy in bwd_x:
        copy.start()

    for copy in fwd_y:
        copy.wait_recv()
    frow[...] = (fwd_part[...] + fwd_in[0] + fwd_in[1] + fwd_in[2]) * (1.0 / 16)

    def fwd_mean(rel, half):
        return frow[lax.rem(y + rel, 4), half:half + 1, :]

    m6, m7 = unfar(fwd_mean(2, 0), fwd_mean(2, 1))
    for chunk, row in enumerate((fwd_mean(0, 0), fwd_mean(0, 1), fwd_mean(3, 0), fwd_mean(1, 1),
                                 fwd_mean(3, 1), fwd_mean(1, 0), m6, m7)):
        fcol[chunk * 128:(chunk + 1) * 128, :] = jnp.transpose(jnp.broadcast_to(row, (128, 128)))

    for copy in bwd_x:
        copy.wait_recv()
    bwd_two2 = (bwd_two[...] + bwd_xin[0] + bwd_xin[1] + bwd_xin[2]) * (1.0 / 16)
    bwd_part2 = tgt_part
    bwd_part2[...] = bwd_two2

    def bwd_mean(rel, i):
        return bwd_part2[lax.rem(x + rel, 4), i:i + 1, :]

    def put_brow(chunk, value):
        brow[:, chunk * 128:(chunk + 1) * 128] = value

    for chunk in range(4):
        put_brow(chunk, bwd_mean(0, chunk))
    for p in range(2):
        put_brow(4 + 2 * p, bwd_mean(3, 2 * p))
        put_brow(5 + 2 * p, bwd_mean(1, 2 * p + 1))
        put_brow(8 + 2 * p, bwd_mean(3, 2 * p + 1))
        put_brow(9 + 2 * p, bwd_mean(1, 2 * p))
        near, distant = unfar(bwd_mean(2, 2 * p), bwd_mean(2, 2 * p + 1))
        put_brow(12 + p, near)
        put_brow(14 + p, distant)

    peaks = (jnp.zeros((8, 128), F32),) * 16
    for chunk_row in range(8):
        rel = ROW_REL[chunk_row]

        def margin_rows(g, peaks):
            at = pl.ds(aligned(chunk_row * 128 + g * 8, 8), 8)
            mean = fcol[at, :]
            best = jnp.zeros((8, 128), F32)
            new = []
            for chunk in range(16):
                cols = slice(chunk * 128, (chunk + 1) * 128)
                margin = (scores[at, cols] * weight[rel, :, cols]) / (mean + brow[:, cols])
                best = jnp.maximum(best, margin)
                new.append(jnp.maximum(peaks[chunk], margin))
            fwd_val[at, :] = best
            return tuple(new)

        peaks = lax.fori_loop(0, 16, margin_rows, peaks, unroll=2)

    def tgt_peak(chunk):
        return jnp.max(peaks[chunk], axis=0, keepdims=True)

    for rel, rows in enumerate(natural_cols(tgt_peak)):
        for i, value in enumerate(rows):
            tgt_part[lax.rem(x + rel, 4), i:i + 1, :] = value
    tgt_x = [remote(tgt_part.at[lax.rem(x + d, 4)], tgt_xin.at[d - 1], 35 + d, x_dev(d))
             for d in range(1, 4)]
    for copy in tgt_x:
        copy.start()

    def src_peak(chunk):
        values = jnp.transpose(fwd_val[chunk * 128:(chunk + 1) * 128, :])
        return jnp.max(values, axis=0, keepdims=True)

    for rel, rows in enumerate(natural_rows(src_peak)):
        for i, value in enumerate(rows):
            src_part[lax.rem(y + rel, 4), i:i + 1, :] = value
    src_y = [remote(src_part.at[lax.rem(y + d, 4)], src_in.at[d - 1], 38 + d, y_dev(d))
             for d in range(1, 4)]
    for copy in src_y:
        copy.start()

    for copy in tgt_x:
        copy.wait_recv()
    tgt_two[...] = jnp.maximum(jnp.maximum(tgt_part[x], tgt_xin[0]),
                               jnp.maximum(tgt_xin[1], tgt_xin[2]))
    tgt_z = [remote(tgt_two, tgt_zin.at[d - 1], 41 + d, zc_dev(d)) for d in range(1, 8)]
    for copy in tgt_z:
        copy.start()
    for copy in src_y:
        copy.wait_recv()
    src_out[...] = jnp.maximum(jnp.maximum(src_part[y], src_in[0]),
                               jnp.maximum(src_in[1], src_in[2]))
    for copy in tgt_z:
        copy.wait_recv()
    best = tgt_two[...]
    for d in range(7):
        best = jnp.maximum(best, tgt_zin[d])
    tgt_out[...] = best

    for copies in (own_copies, idx_copies, far_copies, pass_copies, bwd_z, fwd_y, bwd_x,
                   tgt_x, src_y, tgt_z):
        for copy in copies:
            copy.wait_send()


def body(src_emb, tgt_emb, pair_list, fwd_idx, bwd_idx):
    hbm = pl.BlockSpec(memory_space=pl.ANY)
    vmem = pl.BlockSpec(memory_space=pltpu.VMEM)
    src_best, tgt_best = pl.pallas_call(
        kernel,
        out_shape=(jax.ShapeDtypeStruct((2, 128), F32), jax.ShapeDtypeStruct((4, 128), F32)),
        in_specs=[hbm, hbm, pl.BlockSpec(memory_space=pltpu.SMEM), hbm, hbm],
        out_specs=(vmem, vmem),
        scratch_shapes=[
            pltpu.VMEM((256, D), BF16), pltpu.VMEM((512, D), BF16),
            pltpu.VMEM((1024, D), BF16), pltpu.VMEM((2048, D), BF16),
            pltpu.VMEM((1024, 2048), F32),
            pltpu.VMEM((16, 1024), I32), pltpu.VMEM((4, 16, 512), I32),
            pltpu.VMEM((1024, 128), I32), pltpu.VMEM((16, 2048), I32),
            pltpu.VMEM((1024, 128), F32), pltpu.VMEM((16, 2048), F32),
            pltpu.VMEM((4, 1, 2048), F32),
            pltpu.VMEM((4, 2, 128), F32), pltpu.VMEM((1024, 128), F32),
            pltpu.VMEM((1, 2048), F32),
            pltpu.VMEM((4, 2, 128), F32), pltpu.VMEM((3, 4, 2, 128), F32),
            pltpu.VMEM((4, 4, 128), F32), pltpu.VMEM((7, 4, 4, 128), F32),
            pltpu.VMEM((4, 4, 128), F32), pltpu.VMEM((3, 4, 4, 128), F32),
            pltpu.VMEM((4, 2, 128), F32), pltpu.VMEM((3, 2, 128), F32),
            pltpu.VMEM((4, 4, 128), F32), pltpu.VMEM((3, 4, 128), F32),
            pltpu.VMEM((4, 128), F32), pltpu.VMEM((7, 4, 128), F32),
            pltpu.SemaphoreType.DMA((4,)),
            pltpu.SemaphoreType.DMA((49,)), pltpu.SemaphoreType.DMA((49,)),
        ],
        compiler_params=pltpu.CompilerParams(
            collective_id=0, has_side_effects=True, vmem_limit_bytes=60 << 20),
    )(src_emb, tgt_emb, pair_list.T, fwd_idx.T, bwd_idx.T)
    return src_best.reshape(256), tgt_best.reshape(512)


def solution(mesh):
    return jax.shard_map(
        body,
        mesh=mesh,
        in_specs=(
            P(("src", "tgt"), None),
            P("tgt", None),
            P("src", None),
            P("src", None),
            P("tgt", None),
        ),
        out_specs=(P(("src", "tgt")), P("tgt")),
        check_vma=False,
    )
```

time: 1970 us -> 65.8 us (0.03)
  local copies, waits for them, and re-layouts: 1610 us -> 1.76 us
  blocking collectives: 165 us -> 0 us
  waiting for transfers between devices: 70.4 us -> 0 us
  Pallas kernels: 0 us -> 63.2 us
  matrix products: 50.3 us -> 0 us
  other arithmetic: 46.4 us -> 0 us
  loops' own time: 24.6 us -> 0 us
    gather x96 -> x0, local copies, waits for them, and re-layouts: 1580 us -> none  [the longest x48 1050 us: neighbour_terms(): bwd_value = jnp.take_along_axis(scores.T, bwd_idx % BLOCK, axis=1)]
    pmax x2 -> x0, blocking collectives: 82.4 us -> none  [the longest x1 56.2 us: body(): group_best = lax.pmax(src_peak.reshape(-1), 'tgt')]
    psum x2 -> x0, blocking collectives: 82.2 us -> none  [the longest x1 55.6 us: body(): lax.psum(fwd_part.reshape(-1), 'tgt').reshape(group_blocks, BLOCK)]
    all_gather x1 -> x0, waiting for transfers between devices: 70.3 us -> none  [body(): group_unit = lax.all_gather(src_unit, 'tgt', axis=0, tiled=True)]
    pallas_call x0 -> x1, Pallas kernels: none -> 63.2 us  [body(): pl.pallas_call(kernel, out_shape=(jax.ShapeDtypeStruct((2, 128), F32), ja...]
    dot_general x32 -> x0, matrix products: 50.3 us -> none  [similar(): jnp.einsum('id,jd->ij', rows, tgt_unit, preferred_element_type=jnp.float32)]
    reduce_sum x34 -> x0, other arithmetic: 24.8 us -> none  [the longest x16 17.1 us: neighbour_terms(): fwd_row = jnp.sum(jnp.where(fwd_hit, fwd_value, 0.0), axis=1)]
    another operation x34 -> x0, loops' own time: 24.6 us -> none  [the longest x1 11.3 us: body(): lax.fori_loop(0, group_blocks, first_pass, (jnp.zeros((group_blocks, BLOC...]
  transfers between devices with their start and end apart: 1 -> 0, of which waited for: 1 -> 0; matrix products, arithmetic and copies ran while one was open for 0% -> 0% of each run, Pallas kernels for 0% -> 0%
where the time goes in v1:
time: 65.8 us; the launch traced here: 65.6 us
  Pallas kernels  63.2 us (96%)
  local copies, waits for them, and re-layouts  1.76 us (3%)
  between operations  0.66 us (1%)
    pallas_call x1, Pallas kernels, body(): pl.pallas_call(kernel, out_shape=(jax.ShapeDtypeStruct((2, 128), F32), ja...  63.2 us
    unnamed x6, local copies, waits for them, and re-layouts  1.76 us

profile of v1, /device:TPU:1, one launch (start us, length us, event | category | flops | bytes accessed | tf_op | source)
XLA Modules:
  0.0 65.6 jit_solution(6020593412455219916)
XLA Ops:
  0.6 63.2 %shard_map.68 = (f32[2,128]{1,0:T(2,128)}, f32[4,128]{1,0:T(4,128)}) custom-call(bf16[256,1024]{1,0:T(8,128)(2,1)} %src_hbm.1, bf16[512,1024]{1,0:T(8,128)(2,1)} %tgt_hbm.1, s32[8,16]{1,0:T(8,128)} %bitcast.7, s32[16,4096]{1,0:T(8,128)} %bitcast.5, s32[16,512]{1,0:T(8,128)} %bitcast.6), custom_call_target="tpu_custom_call" | custom-call | tf_op jit(solution)/shard_map/pallas_call | solution.py:449
  63.9 0.0 copy-start.1
  63.9 0.0 copy-start
  63.9 0.6 copy-done.1
  64.5 0.6 copy.9
  65.1 0.0 copy-done
  65.1 0.6 copy.10
Async XLA Ops:
  63.9 0.6 copy-start.1
  63.9 1.2 %copy-start = (f32[4,128]{1,0:T(4,128)S(1)}, f32[4,128]{1,0:T(4,128)}, u32[]{:S(2)}) copy-start(f32[4,128]{1,0:T(4,128)} %get-tuple-element.5) | copy-start | bytes 6148

commit v2 on v1

--- a/solution.py
+++ b/solution.py
@@ -182,50 +182,38 @@
     fwd_val[...] = jnp.zeros((1024, 128), F32)
     bwd_val[...] = jnp.zeros((16, 2048), F32)
 
+    def pick_from(part, index, axis):
+        return jnp.take_along_axis(part, index, axis=axis, mode="promise_in_bounds")
+
     def region(row, rows, col, cols):
-        def dots(i, _):
-            at = pl.ds(aligned(col + i * 256, 256), 256)
-            scores[row:row + rows, at] = lax.dot_general(
-                src_buf[row:row + rows, :], tgt_buf[at, :], (((1,), (1,)), ((), ())),
-                preferred_element_type=F32)
-            return 0
-        lax.fori_loop(0, cols // 256, dots, 0)
-
-        def fwd_rows(g, _):
-            at = pl.ds(aligned(row + g * 8, 8), 8)
-            index = fwd_pos[at, :]
-            pick = index & 127
-            where = index >> 7
-            value = fwd_val[at, :]
-            for chunk in range(col // 128, (col + cols) // 128):
-                found = jnp.take_along_axis(
-                    scores[at, chunk * 128:(chunk + 1) * 128], pick, axis=1,
-                    mode="promise_in_bounds")
-                value = jnp.where(where == chunk, found, value)
-            fwd_val[at, :] = value
-            return 0
-        lax.fori_loop(0, rows // 8, fwd_rows, 0, unroll=4)
-
-        def bwd_cols(i, _):
-            at = pl.ds(aligned(col + i * 128, 128), 128)
-            index0, index1 = bwd_pos[0:8, at], bwd_pos[8:16, at]
-            pick0, pick1 = index0 & 7, index1 & 7
-            where0, where1 = index0 >> 3, index1 >> 3
-
-            def group(g, values):
-                value0, value1 = values
-                here = row // 8 + g
-                part = scores[pl.ds(aligned(row + g * 8, 8), 8), at]
-                found0 = jnp.take_along_axis(part, pick0, axis=0, mode="promise_in_bounds")
-                found1 = jnp.take_along_axis(part, pick1, axis=0, mode="promise_in_bounds")
-                return (jnp.where(where0 == here, found0, value0),
-                        jnp.where(where1 == here, found1, value1))
-            value0, value1 = lax.fori_loop(
-                0, rows // 8, group, (bwd_val[0:8, at], bwd_val[8:16, at]), unroll=16)
-            bwd_val[0:8, at] = value0
-            bwd_val[8:16, at] = value1
-            return 0
-        lax.fori_loop(0, cols // 128, bwd_cols, 0)
+        groups = range(row // 8, (row + rows) // 8)
+        for tile in range(col, col + cols, 256):
+            scores[row:row + rows, tile:tile + 256] = lax.dot_general(
+                src_buf[row:row + rows, :], tgt_buf[tile:tile + 256, :],
+                (((1,), (1,)), ((), ())), preferred_element_type=F32)
+            chunks = (tile // 128, tile // 128 + 1)
+            for chunk in chunks:
+                at = slice(chunk * 128, chunk * 128 + 128)
+                index0, index1 = bwd_pos[0:8, at], bwd_pos[8:16, at]
+                pick0, pick1 = index0 & 7, index1 & 7
+                where0, where1 = index0 >> 3, index1 >> 3
+                value0, value1 = bwd_val[0:8, at], bwd_val[8:16, at]
+                for group in groups:
+                    part = scores[group * 8:group * 8 + 8, at]
+                    value0 = jnp.where(where0 == group, pick_from(part, pick0, 0), value0)
+                    value1 = jnp.where(where1 == group, pick_from(part, pick1, 0), value1)
+                bwd_val[0:8, at] = value0
+                bwd_val[8:16, at] = value1
+            for group in groups:
+                at = slice(group * 8, group * 8 + 8)
+                index = fwd_pos[at, :]
+                pick = index & 127
+                where = index >> 7
+                value = fwd_val[at, :]
+                for chunk in chunks:
+                    part = scores[at, chunk * 128:chunk * 128 + 128]
+                    value = jnp.where(where == chunk, pick_from(part, pick, 1), value)
+                fwd_val[at, :] = value
 
     region(0, 256, 0, 512)
 

time: 65.8 us -> 54.2 us (0.82)
  Pallas kernels: 63.2 us -> 51.6 us
    pallas_call x1, Pallas kernels: 63.2 us -> 51.6 us  [body(): pl.pallas_call(kernel, out_shape=(jax.ShapeDtypeStruct((2, 128), F32), ja...]
where the time goes in v2:
time: 54.2 us; the launch traced here: 54 us
  Pallas kernels  51.6 us (95%)
  local copies, waits for them, and re-layouts  1.76 us (3%)
  between operations  0.66 us (1%)
    pallas_call x1, Pallas kernels, body(): pl.pallas_call(kernel, out_shape=(jax.ShapeDtypeStruct((2, 128), F32), ja...  51.6 us
    unnamed x6, local copies, waits for them, and re-layouts  1.76 us

profile of v2, /device:TPU:1, one launch (start us, length us, event | category | flops | bytes accessed | tf_op | source)
XLA Modules:
  0.0 54.0 jit_solution(17403698518030413643)
XLA Ops:
  0.6 51.6 %shard_map.68 = (f32[2,128]{1,0:T(2,128)}, f32[4,128]{1,0:T(4,128)}) custom-call(bf16[256,1024]{1,0:T(8,128)(2,1)} %src_hbm.1, bf16[512,1024]{1,0:T(8,128)(2,1)} %tgt_hbm.1, s32[8,16]{1,0:T(8,128)} %bitcast.7, s32[16,4096]{1,0:T(8,128)} %bitcast.5, s32[16,512]{1,0:T(8,128)} %bitcast.6), custom_call_target="tpu_custom_call" | custom-call | tf_op jit(solution)/shard_map/pallas_call | solution.py:437
  52.2 0.0 copy-start.1
  52.2 0.0 copy-start
  52.2 0.6 %copy-done.1 = f32[2,128]{1,0:T(2,128)S(1)} copy-done((f32[2,128]{1,0:T(2,128)S(1)}, f32[2,128]{1,0:T(2,128)}, u32[]{:S(2)}) %copy-start.1) | copy-done | bytes 1048
  52.9 0.6 %copy.9 = f32[256]{0:T(256)} copy(f32[256]{0:T(256)S(1)} %bitcast.9) | data formatting | bytes 2048
  53.4 0.0 copy-done
  53.4 0.6 %copy.10 = f32[512]{0:T(512)} copy(f32[512]{0:T(512)S(1)} %bitcast.8) | data formatting | bytes 4096
Async XLA Ops:
  52.2 0.6 %copy-start.1 = (f32[2,128]{1,0:T(2,128)S(1)}, f32[2,128]{1,0:T(2,128)}, u32[]{:S(2)}) copy-start(f32[2,128]{1,0:T(2,128)} %get-tuple-element.4) | copy-start | bytes 3076
  52.2 1.2 %copy-start = (f32[4,128]{1,0:T(4,128)S(1)}, f32[4,128]{1,0:T(4,128)}, u32[]{:S(2)}) copy-start(f32[4,128]{1,0:T(4,128)} %get-tuple-element.5) | copy-start | bytes 6148

commit v3 on v2

--- a/solution.py
+++ b/solution.py
@@ -24,7 +24,7 @@
            src_raw, tgt_raw, src_buf, tgt_buf, scores, fwd_raw, bwd_raw, fwd_pos, bwd_pos,
            fwd_val, bwd_val, weight, frow, fcol, brow, fwd_part, fwd_in, bwd_part, bwd_zin,
            bwd_two, bwd_xin, src_part, src_in, tgt_part, tgt_xin, tgt_two, tgt_zin,
-           load_sem, send_sem, recv_sem):
+           load_sem, send_sem, recv_sem, ready_sem):
     s = lax.axis_index("src")
     t = lax.axis_index("tgt")
     core = lax.rem(s, 2)
@@ -53,11 +53,8 @@
     fwd_load.start()
 
     barrier = pltpu.get_barrier_semaphore()
-    for d in (1, 2, 3):
-        pl.semaphore_signal(barrier, inc=1, device_id=y_dev(d), device_id_type=MESH)
-        pl.semaphore_signal(barrier, inc=1, device_id=x_dev(d), device_id_type=MESH)
-    for d in range(1, 8):
-        pl.semaphore_signal(barrier, inc=1, device_id=zc_dev(d), device_id_type=MESH)
+    for device in (y_dev(1), y_dev(3), x_dev(1), x_dev(3), zc_dev(1), zc_dev(2), zc_dev(6)):
+        pl.semaphore_signal(barrier, inc=1, device_id=device, device_id_type=MESH)
 
     def remote(src, dst, sem, device):
         return pltpu.make_async_remote_copy(
@@ -78,7 +75,7 @@
     normalise(src_raw, src_buf, 0, 0, 256)
     tgt_load.wait()
     normalise(tgt_raw, tgt_buf, c256, c256, 256)
-    pl.semaphore_wait(barrier, 13)
+    pl.semaphore_wait(barrier, 7)
 
     def srow(first, count):
         return src_buf.at[pl.ds(first, count), :]
@@ -96,17 +93,20 @@
         remote(trow(c256 + 128, 128), trow(1024 + c256, 128), 6, x_dev(1)),
         remote(trow(c256, 128), trow(1152 + c256, 128), 7, x_dev(3)),
     )
+    idx_cols = pl.ds(aligned(c256, 256), 256)
     idx_copies = (
-        remote(bwd_hbm, bwd_raw.at[3], 8, x_dev(1)),
-        remote(bwd_hbm, bwd_raw.at[1], 9, x_dev(3)),
-        remote(bwd_hbm, bwd_raw.at[2], 10, x_dev(2)),
+        remote(bwd_hbm.at[:, idx_cols], bwd_raw.at[3, :, idx_cols], 8, x_dev(1)),
+        remote(bwd_hbm.at[:, idx_cols], bwd_raw.at[1, :, idx_cols], 9, x_dev(3)),
+        remote(bwd_raw.at[3, :, idx_cols], bwd_raw.at[2, :, idx_cols], 10, x_dev(1)),
     )
     for copy in own_copies[:4]:
         copy.start()
-    for copy in idx_copies:
+    for copy in idx_copies[:2]:
         copy.start()
     for copy in own_copies[4:]:
         copy.start()
+    for device in (zc_dev(2), zc_dev(6)):
+        pl.semaphore_signal(ready_sem, inc=1, device_id=device, device_id_type=MESH)
 
     normalise(tgt_raw, tgt_buf, 256 - c256, 256 - c256, 256)
 
@@ -183,7 +183,19 @@
     bwd_val[...] = jnp.zeros((16, 2048), F32)
 
     def pick_from(part, index, axis):
-        return jnp.take_along_axis(part, index, axis=axis, mode="promise_in_bounds")
+        other = (1 - axis,)
+        numbers = lax.GatherDimensionNumbers(
+            offset_dims=(), collapsed_slice_dims=(axis,), start_index_map=(axis,),
+            operand_batching_dims=other, start_indices_batching_dims=other)
+        return lax.gather(part, index, numbers, (1, 1),
+                          mode=lax.GatherScatterMode.PROMISE_IN_BOUNDS)
+
+    def splat(value):
+        return lax.full((8, 128), value, I32)
+
+    def split(index, mask, shift):
+        pick = lax.bitwise_and(index, splat(mask))
+        return lax.expand_dims(pick, (2,)), lax.shift_right_arithmetic(index, splat(shift))
 
     def region(row, rows, col, cols):
         groups = range(row // 8, (row + rows) // 8)
@@ -194,31 +206,30 @@
             chunks = (tile // 128, tile // 128 + 1)
             for chunk in chunks:
                 at = slice(chunk * 128, chunk * 128 + 128)
-                index0, index1 = bwd_pos[0:8, at], bwd_pos[8:16, at]
-                pick0, pick1 = index0 & 7, index1 & 7
-                where0, where1 = index0 >> 3, index1 >> 3
+                pick0, where0 = split(bwd_pos[0:8, at], 7, 3)
+                pick1, where1 = split(bwd_pos[8:16, at], 7, 3)
                 value0, value1 = bwd_val[0:8, at], bwd_val[8:16, at]
                 for group in groups:
                     part = scores[group * 8:group * 8 + 8, at]
-                    value0 = jnp.where(where0 == group, pick_from(part, pick0, 0), value0)
-                    value1 = jnp.where(where1 == group, pick_from(part, pick1, 0), value1)
+                    here = splat(group)
+                    value0 = lax.select(lax.eq(where0, here), pick_from(part, pick0, 0), value0)
+                    value1 = lax.select(lax.eq(where1, here), pick_from(part, pick1, 0), value1)
                 bwd_val[0:8, at] = value0
                 bwd_val[8:16, at] = value1
             for group in groups:
                 at = slice(group * 8, group * 8 + 8)
-                index = fwd_pos[at, :]
-                pick = index & 127
-                where = index >> 7
+                pick, where = split(fwd_pos[at, :], 127, 7)
                 value = fwd_val[at, :]
                 for chunk in chunks:
                     part = scores[at, chunk * 128:chunk * 128 + 128]
-                    value = jnp.where(where == chunk, pick_from(part, pick, 1), value)
+                    value = lax.select(lax.eq(where, splat(chunk)), pick_from(part, pick, 1), value)
                 fwd_val[at, :] = value
 
     region(0, 256, 0, 512)
 
-    for copy in own_copies[:4]:
-        copy.wait_recv()
+    for copy in own_copies[:4] + idx_copies[:2]:
+        copy.wait_recv()
+    idx_copies[2].start()
     far_copies = (
         remote(srow(256, 64), srow(768, 64), 11, y_dev(1)),
         remote(srow(448, 64), srow(832, 64), 12, y_dev(3)),
@@ -231,47 +242,69 @@
     )
     for copy in far_copies:
         copy.start()
+    pl.semaphore_wait(ready_sem, 2)
     partner = zc_dev(1)
+
+    def passed(first, count, sem):
+        return remote(trow(first, count), trow(first, count), sem, partner)
+
+    def passed_idx(rel, sem):
+        piece = bwd_raw.at[rel, :, idx_cols]
+        return remote(piece, piece, sem, partner)
+
     pass_copies = (
-        remote(trow(512 + c256, 256), trow(512 + c256, 256), 19, partner),
-        remote(trow(1024 + c256, 256), trow(1024 + c256, 256), 20, partner),
-        remote(trow(1536 + c128, 128), trow(1536 + c128, 128), 21, partner),
-        remote(trow(1792 + c128, 128), trow(1792 + c128, 128), 22, partner),
+        passed(512 + c256, 256, 19), passed(1024 + c256, 256, 20),
+        passed(1536 + c128, 64, 21), passed(1600 + c128, 64, 22),
+        passed(1856 + c128, 64, 23), passed(1792 + c128, 64, 24),
+        passed_idx(3, 25), passed_idx(1, 26), passed_idx(2, 27),
     )
+    pass_copies[6].start()
+    pass_copies[7].start()
     pass_copies[0].start()
-    for copy in idx_copies:
-        copy.wait_recv()
+    region(256, 256, 0, 512)
+    pass_copies[6].wait_recv()
+    pass_copies[7].wait_recv()
     for p in range(2):
         bwd_put(4 + 2 * p, bwd_half(3, p, 0))
         bwd_put(5 + 2 * p, bwd_half(1, p, 1))
         bwd_put(8 + 2 * p, bwd_half(3, p, 1))
         bwd_put(9 + 2 * p, bwd_half(1, p, 0))
+    pass_copies[0].wait_recv()
+    region(0, 512, 512, 512)
+
+    for copy in own_copies[4:] + idx_copies[2:]:
+        copy.wait_recv()
+    pass_copies[1].start()
+    pass_copies[8].start()
+    region(512, 256, 0, 1024)
+    pass_copies[1].wait_recv()
+    pass_copies[8].wait_recv()
+    for p in range(2):
         near, distant = far(bwd_half(2, p, 0), bwd_half(2, p, 1))
         bwd_put(12 + p, near)
         bwd_put(14 + p, distant)
-    pass_copies[0].wait_recv()
-    region(0, 256, 512, 512)
-    region(256, 256, 0, 1024)
-
-    for copy in own_copies[4:]:
-        copy.wait_recv()
-    pass_copies[1].start()
-    region(512, 256, 0, 1024)
-    pass_copies[1].wait_recv()
     region(0, 768, 1024, 512)
 
-    for copy in far_copies[:4]:
-        copy.wait_recv()
+    far_copies[2].wait_recv()
     pass_copies[2].start()
+    far_copies[3].wait_recv()
+    pass_copies[3].start()
+    far_copies[0].wait_recv()
+    far_copies[1].wait_recv()
     region(768, 128, 0, 1536)
     pass_copies[2].wait_recv()
+    pass_copies[3].wait_recv()
     region(0, 896, 1536, 256)
 
-    for copy in far_copies[4:]:
-        copy.wait_recv()
-    pass_copies[3].start()
+    far_copies[6].wait_recv()
+    pass_copies[4].start()
+    far_copies[7].wait_recv()
+    pass_copies[5].start()
+    far_copies[4].wait_recv()
+    far_copies[5].wait_recv()
     region(896, 128, 0, 1792)
-    pass_copies[3].wait_recv()
+    pass_copies[4].wait_recv()
+    pass_copies[5].wait_recv()
     region(0, 1024, 1792, 256)
 
     lane1 = lane[0:1, :]
@@ -280,6 +313,8 @@
         return jnp.sum(bwd_val[:, chunk * 128:(chunk + 1) * 128], axis=0, keepdims=True)
 
     def unfar(first, second):
+        if first is None:
+            return None, None
         return jnp.where(lane1 < 64, first, second), jnp.where(lane1 < 64, second, first)
 
     def natural_cols(get):
@@ -305,7 +340,7 @@
     for rel, rows in enumerate(natural_cols(bwd_sum)):
         for i, value in enumerate(rows):
             bwd_part[lax.rem(x + rel, 4), i:i + 1, :] = value
-    bwd_z = [remote(bwd_part, bwd_zin.at[d - 1], 22 + d, zc_dev(d)) for d in range(1, 8)]
+    bwd_z = [remote(bwd_part, bwd_zin.at[d - 1], 27 + d, zc_dev(d)) for d in range(1, 8)]
     for copy in bwd_z:
         copy.start()
 
@@ -316,7 +351,7 @@
     for rel, rows in enumerate(natural_rows(fwd_sum)):
         for i, value in enumerate(rows):
             fwd_part[lax.rem(y + rel, 4), i:i + 1, :] = value
-    fwd_y = [remote(fwd_part, fwd_in.at[d - 1], 29 + d, y_dev(d)) for d in range(1, 4)]
+    fwd_y = [remote(fwd_part, fwd_in.at[d - 1], 34 + d, y_dev(d)) for d in range(1, 4)]
     for copy in fwd_y:
         copy.start()
 
@@ -326,7 +361,7 @@
     for d in range(7):
         total = total + bwd_zin[d]
     bwd_two[...] = total
-    bwd_x = [remote(bwd_two, bwd_xin.at[d - 1], 32 + d, x_dev(d)) for d in range(1, 4)]
+    bwd_x = [remote(bwd_two, bwd_xin.at[d - 1], 37 + d, x_dev(d)) for d in range(1, 4)]
     for copy in bwd_x:
         copy.start()
 
@@ -365,35 +400,41 @@
         put_brow(12 + p, near)
         put_brow(14 + p, distant)
 
-    peaks = (jnp.zeros((8, 128), F32),) * 16
-    for chunk_row in range(8):
-        rel = ROW_REL[chunk_row]
-
-        def margin_rows(g, peaks):
-            at = pl.ds(aligned(chunk_row * 128 + g * 8, 8), 8)
-            mean = fcol[at, :]
-            best = jnp.zeros((8, 128), F32)
-            new = []
-            for chunk in range(16):
-                cols = slice(chunk * 128, (chunk + 1) * 128)
-                margin = (scores[at, cols] * weight[rel, :, cols]) / (mean + brow[:, cols])
-                best = jnp.maximum(best, margin)
-                new.append(jnp.maximum(peaks[chunk], margin))
-            fwd_val[at, :] = best
-            return tuple(new)
-
-        peaks = lax.fori_loop(0, 16, margin_rows, peaks, unroll=2)
-
-    def tgt_peak(chunk):
-        return jnp.max(peaks[chunk], axis=0, keepdims=True)
-
-    for rel, rows in enumerate(natural_cols(tgt_peak)):
-        for i, value in enumerate(rows):
-            tgt_part[lax.rem(x + rel, 4), i:i + 1, :] = value
-    tgt_x = [remote(tgt_part.at[lax.rem(x + d, 4)], tgt_xin.at[d - 1], 35 + d, x_dev(d))
+    def margins(chunks, unroll, first):
+        peaks = (jnp.zeros((8, 128), F32),) * len(chunks)
+        for chunk_row in range(8):
+            rel = ROW_REL[chunk_row]
+
+            def margin_rows(g, peaks):
+                at = pl.ds(aligned(chunk_row * 128 + g * 8, 8), 8)
+                mean = fcol[at, :]
+                best = jnp.zeros((8, 128), F32) if first else fwd_val[at, :]
+                new = []
+                for peak, chunk in zip(peaks, chunks):
+                    cols = slice(chunk * 128, (chunk + 1) * 128)
+                    margin = (scores[at, cols] * weight[rel, :, cols]) / (mean + brow[:, cols])
+                    best = jnp.maximum(best, margin)
+                    new.append(jnp.maximum(peak, margin))
+                fwd_val[at, :] = best
+                return tuple(new)
+
+            peaks = lax.fori_loop(0, 16, margin_rows, peaks, unroll=unroll)
+        return {chunk: jnp.max(peak, axis=0, keepdims=True) for chunk, peak in zip(chunks, peaks)}
+
+    def put_peaks(peaks):
+        for rel, rows in enumerate(natural_cols(peaks.get)):
+            for i, value in enumerate(rows):
+                if value is not None:
+                    tgt_part[lax.rem(x + rel, 4), i:i + 1, :] = value
+
+    put_peaks(margins(range(4, 16), 4, True))
+    tgt_x = [remote(tgt_part.at[lax.rem(x + d, 4)], tgt_xin.at[d - 1], 40 + d, x_dev(d))
              for d in range(1, 4)]
     for copy in tgt_x:
         copy.start()
+    own_peaks = margins(range(4), 8, False)
+    for chunk, value in own_peaks.items():
+        tgt_two[chunk:chunk + 1, :] = value
 
     def src_peak(chunk):
         values = jnp.transpose(fwd_val[chunk * 128:(chunk + 1) * 128, :])
@@ -402,16 +443,16 @@
     for rel, rows in enumerate(natural_rows(src_peak)):
         for i, value in enumerate(rows):
             src_part[lax.rem(y + rel, 4), i:i + 1, :] = value
-    src_y = [remote(src_part.at[lax.rem(y + d, 4)], src_in.at[d - 1], 38 + d, y_dev(d))
+    src_y = [remote(src_part.at[lax.rem(y + d, 4)], src_in.at[d - 1], 43 + d, y_dev(d))
              for d in range(1, 4)]
     for copy in src_y:
         copy.start()
 
     for copy in tgt_x:
         copy.wait_recv()
-    tgt_two[...] = jnp.maximum(jnp.maximum(tgt_part[x], tgt_xin[0]),
+    tgt_two[...] = jnp.maximum(jnp.maximum(tgt_two[...], tgt_xin[0]),
                                jnp.maximum(tgt_xin[1], tgt_xin[2]))
-    tgt_z = [remote(tgt_two, tgt_zin.at[d - 1], 41 + d, zc_dev(d)) for d in range(1, 8)]
+    tgt_z = [remote(tgt_two, tgt_zin.at[d - 1], 46 + d, zc_dev(d)) for d in range(1, 8)]
     for copy in tgt_z:
         copy.start()
     for copy in src_y:
@@ -456,12 +497,23 @@
             pltpu.VMEM((4, 4, 128), F32), pltpu.VMEM((3, 4, 128), F32),
             pltpu.VMEM((4, 128), F32), pltpu.VMEM((7, 4, 128), F32),
             pltpu.SemaphoreType.DMA((4,)),
-            pltpu.SemaphoreType.DMA((49,)), pltpu.SemaphoreType.DMA((49,)),
+            pltpu.SemaphoreType.DMA((54,)), pltpu.SemaphoreType.DMA((54,)),
+            pltpu.SemaphoreType.REGULAR,
         ],
         compiler_params=pltpu.CompilerParams(
             collective_id=0, has_side_effects=True, vmem_limit_bytes=60 << 20),
     )(src_emb, tgt_emb, pair_list.T, fwd_idx.T, bwd_idx.T)
-    return src_best.reshape(256), tgt_best.reshape(512)
+
+    def flatten(src_ref, tgt_ref, src_flat, tgt_flat):
+        src_flat[...] = src_ref[...].reshape(256)
+        tgt_flat[...] = tgt_ref[...].reshape(512)
+
+    return pl.pallas_call(
+        flatten,
+        out_shape=(jax.ShapeDtypeStruct((256,), F32), jax.ShapeDtypeStruct((512,), F32)),
+        in_specs=[vmem, vmem],
+        out_specs=(vmem, vmem),
+    )(src_best, tgt_best)
 
 
 def solution(mesh):

time: 54.2 us -> 52 us (0.959)
  local copies, waits for them, and re-layouts: 1.76 us -> 0 us
    unnamed x6 -> x0, local copies, waits for them, and re-layouts: 1.76 us -> none
    pallas_call x1, Pallas kernels: 51.6 us -> 49.9 us  [body(): pl.pallas_call(kernel, out_shape=(jax.ShapeDtypeStruct((2, 128), F32), ja...]
    pallas_call x0 -> x1, Pallas kernels: none -> 1.27 us  [body(): pl.pallas_call(flatten, out_shape=(jax.ShapeDtypeStruct((256,), F32), jax...]
where the time goes in v3:
time: 52 us; the launch traced here: 51.8 us
  Pallas kernels  51.2 us (98%)
  between operations  0.64 us (1%)
    pallas_call x1, Pallas kernels, body(): pl.pallas_call(kernel, out_shape=(jax.ShapeDtypeStruct((2, 128), F32), ja...  49.9 us
    pallas_call x1, Pallas kernels, body(): pl.pallas_call(flatten, out_shape=(jax.ShapeDtypeStruct((256,), F32), jax...  1.27 us

profile of v3, /device:TPU:1, one launch (start us, length us, event | category | flops | bytes accessed | tf_op | source)
XLA Modules:
  0.0 51.8 jit_solution(13474350083310875372)
XLA Ops:
  0.6 49.9 %shard_map.68 = (f32[2,128]{1,0:T(2,128)}, f32[4,128]{1,0:T(4,128)}) custom-call(bf16[256,1024]{1,0:T(8,128)(2,1)} %src_hbm.1, bf16[512,1024]{1,0:T(8,128)(2,1)} %tgt_hbm.1, s32[8,16]{1,0:T(8,128)} %bitcast.5, s32[16,4096]{1,0:T(8,128)} %bitcast.3, s32[16,512]{1,0:T(8,128)} %bitcast.4), custom_call_target="tpu_custom_call" | custom-call | tf_op jit(solution)/shard_map/pallas_call | solution.py:478
  50.6 1.3 %shard_map.69 = (f32[256]{0:T(256)}, f32[512]{0:T(512)}) custom-call(f32[2,128]{1,0:T(2,128)} %get-tuple-element.4.src_ref, f32[4,128]{1,0:T(4,128)} %get-tuple-element.5.tgt_ref), custom_call_target="tpu_custom_call" | custom-call | tf_op jit(solution)/shard_map/pallas_call | solution.py:511

commit v4 on v3

--- a/solution.py
+++ b/solution.py
@@ -20,10 +20,10 @@
     return pl.multiple_of(value, step)
 
 
-def kernel(src_hbm, tgt_hbm, pair_ref, fwd_hbm, bwd_hbm, src_out, tgt_out,
+def kernel(src_hbm, tgt_hbm, pair_hbm, fwd_hbm, bwd_hbm, src_out, tgt_out, pair_ref,
            src_raw, tgt_raw, src_buf, tgt_buf, scores, fwd_raw, bwd_raw, fwd_pos, bwd_pos,
            fwd_val, bwd_val, weight, frow, fcol, brow, fwd_part, fwd_in, bwd_part, bwd_zin,
-           bwd_two, bwd_xin, src_part, src_in, tgt_part, tgt_xin, tgt_two, tgt_zin,
+           bwd_two, bwd_xin, src_part, src_in, tgt_part, tgt_own, tgt_in, tgt_two, tgt_other,
            load_sem, send_sem, recv_sem, ready_sem):
     s = lax.axis_index("src")
     t = lax.axis_index("tgt")
@@ -51,6 +51,8 @@
     fwd_load = pltpu.make_async_copy(
         fwd_hbm.at[:, pl.ds(aligned(x * 1024, 1024), 1024)], fwd_raw, load_sem.at[3])
     fwd_load.start()
+    pair_load = pltpu.make_async_copy(pair_hbm, pair_ref, load_sem.at[4])
+    pair_load.start()
 
     barrier = pltpu.get_barrier_semaphore()
     for device in (y_dev(1), y_dev(3), x_dev(1), x_dev(3), zc_dev(1), zc_dev(2), zc_dev(6)):
@@ -125,6 +127,7 @@
                         weight[rel, :, chunk * 128:(chunk + 1) * 128] = value
         return 0
 
+    pair_load.wait()
     lax.fori_loop(0, 4, weight_row, 0)
 
     lane = lax.broadcasted_iota(I32, (16, 128), 1)
@@ -296,13 +299,14 @@
     pass_copies[3].wait_recv()
     region(0, 896, 1536, 256)
 
+    far_copies[4].wait_recv()
+    far_copies[5].wait_recv()
+    region(896, 128, 0, 1024)
     far_copies[6].wait_recv()
     pass_copies[4].start()
     far_copies[7].wait_recv()
     pass_copies[5].start()
-    far_copies[4].wait_recv()
-    far_copies[5].wait_recv()
-    region(896, 128, 0, 1792)
+    region(896, 128, 1024, 768)
     pass_copies[4].wait_recv()
     pass_copies[5].wait_recv()
     region(0, 1024, 1792, 256)
@@ -428,13 +432,21 @@
                     tgt_part[lax.rem(x + rel, 4), i:i + 1, :] = value
 
     put_peaks(margins(range(4, 16), 4, True))
-    tgt_x = [remote(tgt_part.at[lax.rem(x + d, 4)], tgt_xin.at[d - 1], 40 + d, x_dev(d))
-             for d in range(1, 4)]
-    for copy in tgt_x:
-        copy.start()
-    own_peaks = margins(range(4), 8, False)
-    for chunk, value in own_peaks.items():
-        tgt_two[chunk:chunk + 1, :] = value
+    def tgt_send(piece, dx, dz):
+        device = (2 * lax.rem(z + dz, 4) + core, 4 * lax.rem(x + dx, 4) + y)
+        place = 4 * dx + dz - 1
+        return remote(piece, tgt_in.at[place], 41 + place, device)
+
+    tgt_copies = [tgt_send(tgt_part.at[lax.rem(x + dx, 4)], dx, dz)
+                  for dz in range(4) for dx in (2, 1, 3)]
+    for copy in tgt_copies:
+        copy.start()
+    for chunk, value in margins(range(4), 8, False).items():
+        tgt_own[chunk:chunk + 1, :] = value
+    own_sends = [tgt_send(tgt_own, 0, dz) for dz in (2, 1, 3)]
+    for copy in own_sends:
+        copy.start()
+    tgt_copies += own_sends
 
     def src_peak(chunk):
         values = jnp.transpose(fwd_val[chunk * 128:(chunk + 1) * 128, :])
@@ -443,31 +455,28 @@
     for rel, rows in enumerate(natural_rows(src_peak)):
         for i, value in enumerate(rows):
             src_part[lax.rem(y + rel, 4), i:i + 1, :] = value
-    src_y = [remote(src_part.at[lax.rem(y + d, 4)], src_in.at[d - 1], 43 + d, y_dev(d))
+    src_y = [remote(src_part.at[lax.rem(y + d, 4)], src_in.at[d - 1], 56 + d, y_dev(d))
              for d in range(1, 4)]
     for copy in src_y:
         copy.start()
 
-    for copy in tgt_x:
-        copy.wait_recv()
-    tgt_two[...] = jnp.maximum(jnp.maximum(tgt_two[...], tgt_xin[0]),
-                               jnp.maximum(tgt_xin[1], tgt_xin[2]))
-    tgt_z = [remote(tgt_two, tgt_zin.at[d - 1], 46 + d, zc_dev(d)) for d in range(1, 8)]
-    for copy in tgt_z:
-        copy.start()
+    for copy in tgt_copies:
+        copy.wait_recv()
+    best = tgt_own[...]
+    for place in range(15):
+        best = jnp.maximum(best, tgt_in[place])
+    tgt_two[...] = best
+    tgt_core = remote(tgt_two, tgt_other, 56, partner)
+    tgt_core.start()
     for copy in src_y:
         copy.wait_recv()
     src_out[...] = jnp.maximum(jnp.maximum(src_part[y], src_in[0]),
                                jnp.maximum(src_in[1], src_in[2]))
-    for copy in tgt_z:
-        copy.wait_recv()
-    best = tgt_two[...]
-    for d in range(7):
-        best = jnp.maximum(best, tgt_zin[d])
-    tgt_out[...] = best
+    tgt_core.wait_recv()
+    tgt_out[...] = jnp.maximum(best, tgt_other[...])
 
     for copies in (own_copies, idx_copies, far_copies, pass_copies, bwd_z, fwd_y, bwd_x,
-                   tgt_x, src_y, tgt_z):
+                   tgt_copies, src_y, (tgt_core,)):
         for copy in copies:
             copy.wait_send()
 
@@ -478,9 +487,10 @@
     src_best, tgt_best = pl.pallas_call(
         kernel,
         out_shape=(jax.ShapeDtypeStruct((2, 128), F32), jax.ShapeDtypeStruct((4, 128), F32)),
-        in_specs=[hbm, hbm, pl.BlockSpec(memory_space=pltpu.SMEM), hbm, hbm],
+        in_specs=[hbm] * 5,
         out_specs=(vmem, vmem),
         scratch_shapes=[
+            pltpu.SMEM((8, 16), I32),
             pltpu.VMEM((256, D), BF16), pltpu.VMEM((512, D), BF16),
             pltpu.VMEM((1024, D), BF16), pltpu.VMEM((2048, D), BF16),
             pltpu.VMEM((1024, 2048), F32),
@@ -494,10 +504,10 @@
             pltpu.VMEM((4, 4, 128), F32), pltpu.VMEM((7, 4, 4, 128), F32),
             pltpu.VMEM((4, 4, 128), F32), pltpu.VMEM((3, 4, 4, 128), F32),
             pltpu.VMEM((4, 2, 128), F32), pltpu.VMEM((3, 2, 128), F32),
-            pltpu.VMEM((4, 4, 128), F32), pltpu.VMEM((3, 4, 128), F32),
-            pltpu.VMEM((4, 128), F32), pltpu.VMEM((7, 4, 128), F32),
-            pltpu.SemaphoreType.DMA((4,)),
-            pltpu.SemaphoreType.DMA((54,)), pltpu.SemaphoreType.DMA((54,)),
+            pltpu.VMEM((4, 4, 128), F32), pltpu.VMEM((4, 128), F32),
+            pltpu.VMEM((15, 4, 128), F32), pltpu.VMEM((4, 128), F32), pltpu.VMEM((4, 128), F32),
+            pltpu.SemaphoreType.DMA((5,)),
+            pltpu.SemaphoreType.DMA((60,)), pltpu.SemaphoreType.DMA((60,)),
             pltpu.SemaphoreType.REGULAR,
         ],
         compiler_params=pltpu.CompilerParams(

time: 52 us -> 51.3 us (0.987)
  Pallas kernels: 51.2 us -> 50.5 us
    pallas_call x1, Pallas kernels: 49.9 us -> 49.2 us  [body(): pl.pallas_call(kernel, out_shape=(jax.ShapeDtypeStruct((2, 128), F32), ja...]
where the time goes in v4:
time: 51.3 us; the launch traced here: 51.1 us
  Pallas kernels  50.5 us (98%)
  between operations  0.64 us (1%)
    pallas_call x1, Pallas kernels, body(): pl.pallas_call(kernel, out_shape=(jax.ShapeDtypeStruct((2, 128), F32), ja...  49.2 us
    pallas_call x1, Pallas kernels, body(): pl.pallas_call(flatten, out_shape=(jax.ShapeDtypeStruct((256,), F32), jax...  1.27 us

profile of v4, /device:TPU:1, one launch (start us, length us, event | category | flops | bytes accessed | tf_op | source)
XLA Modules:
  0.0 51.1 jit_solution(1260636434637492993)
XLA Ops:
  0.6 49.2 %shard_map.68 = (f32[2,128]{1,0:T(2,128)}, f32[4,128]{1,0:T(4,128)}) custom-call(bf16[256,1024]{1,0:T(8,128)(2,1)} %src_hbm.1, bf16[512,1024]{1,0:T(8,128)(2,1)} %tgt_hbm.1, s32[8,16]{1,0:T(8,128)} %bitcast.5, s32[16,4096]{1,0:T(8,128)} %bitcast.3, s32[16,512]{1,0:T(8,128)} %bitcast.4), custom_call_target="tpu_custom_call" | custom-call | tf_op jit(solution)/shard_map/pallas_call | solution.py:487
  49.8 1.3 %shard_map.69 = (f32[256]{0:T(256)}, f32[512]{0:T(512)}) custom-call(f32[2,128]{1,0:T(2,128)} %get-tuple-element.4.src_ref, f32[4,128]{1,0:T(4,128)} %get-tuple-element.5.tgt_ref), custom_call_target="tpu_custom_call" | custom-call | tf_op jit(solution)/shard_map/pallas_call | solution.py:521

commit v5 on v4

--- a/solution.py
+++ b/solution.py
@@ -11,7 +11,6 @@
 BF16 = jnp.bfloat16
 I32 = jnp.int32
 
-ROW_REL = (0, 0, 3, 1, 3, 1, 2, 2)
 COL_SLOT = ((0, 0), (0, 0), (0, 1), (0, 1), (3, 0), (1, 0), (3, 1), (1, 1),
             (3, 0), (1, 0), (3, 1), (1, 1), (2, 0), (2, 1), (2, 0), (2, 1))
 
@@ -22,7 +21,7 @@
 
 def kernel(src_hbm, tgt_hbm, pair_hbm, fwd_hbm, bwd_hbm, src_out, tgt_out, pair_ref,
            src_raw, tgt_raw, src_buf, tgt_buf, scores, fwd_raw, bwd_raw, fwd_pos, bwd_pos,
-           fwd_val, bwd_val, weight, frow, fcol, brow, fwd_part, fwd_in, bwd_part, bwd_zin,
+           fwd_val, bwd_val, weight, frow, rowform, fcol, brow, fwd_part, fwd_in, bwd_part, bwd_zin,
            bwd_two, bwd_xin, src_part, src_in, tgt_part, tgt_own, tgt_in, tgt_two, tgt_other,
            load_sem, send_sem, recv_sem, ready_sem):
     s = lax.axis_index("src")
@@ -112,7 +111,8 @@
 
     normalise(tgt_raw, tgt_buf, 256 - c256, 256 - c256, 256)
 
-    def weight_row(rel, _):
+    def weight_row(kind, _):
+        rel = lax.select(kind < 2, 0, lax.select(kind >= 6, 2, lax.select(kind % 2 == 0, 3, 1)))
         row = 4 * x + lax.rem(y + rel, 4)
         names = [pair_ref[k, row] for k in range(8)]
         for relx in range(4):
@@ -124,11 +124,11 @@
                 value = jnp.full((1, 128), jnp.where(hit > 0, 2.0, 0.0), F32)
                 for chunk in range(16):
                     if COL_SLOT[chunk] == (relx, p):
-                        weight[rel, :, chunk * 128:(chunk + 1) * 128] = value
+                        weight[kind, :, chunk * 128:(chunk + 1) * 128] = value
         return 0
 
     pair_load.wait()
-    lax.fori_loop(0, 4, weight_row, 0)
+    lax.fori_loop(0, 8, weight_row, 0)
 
     lane = lax.broadcasted_iota(I32, (16, 128), 1)
 
@@ -292,21 +292,18 @@
     pass_copies[2].start()
     far_copies[3].wait_recv()
     pass_copies[3].start()
-    far_copies[0].wait_recv()
-    far_copies[1].wait_recv()
-    region(768, 128, 0, 1536)
     pass_copies[2].wait_recv()
     pass_copies[3].wait_recv()
-    region(0, 896, 1536, 256)
-
-    far_copies[4].wait_recv()
-    far_copies[5].wait_recv()
-    region(896, 128, 0, 1024)
+    region(0, 768, 1536, 256)
+
+    for copy in far_copies[:2] + far_copies[4:6]:
+        copy.wait_recv()
+    region(768, 256, 0, 768)
     far_copies[6].wait_recv()
     pass_copies[4].start()
     far_copies[7].wait_recv()
     pass_copies[5].start()
-    region(896, 128, 1024, 768)
+    region(768, 256, 768, 1024)
     pass_copies[4].wait_recv()
     pass_copies[5].wait_recv()
     region(0, 1024, 1792, 256)
@@ -348,11 +345,18 @@
     for copy in bwd_z:
         copy.start()
 
-    def fwd_sum(chunk):
-        values = jnp.transpose(fwd_val[chunk * 128:(chunk + 1) * 128, :])
-        return jnp.sum(values[0:16, :], axis=0, keepdims=True)
-
-    for rel, rows in enumerate(natural_rows(fwd_sum)):
+    def to_rows(combine):
+        def step(chunk, _):
+            at = pl.ds(aligned(chunk * 128, 128), 128)
+            rowform[chunk] = combine(jnp.transpose(fwd_val[at, :]))
+            return 0
+        lax.fori_loop(0, 8, step, 0)
+
+    def row_of(chunk):
+        return rowform[chunk]
+
+    to_rows(lambda values: jnp.sum(values[0:16, :], axis=0, keepdims=True))
+    for rel, rows in enumerate(natural_rows(row_of)):
         for i, value in enumerate(rows):
             fwd_part[lax.rem(y + rel, 4), i:i + 1, :] = value
     fwd_y = [remote(fwd_part, fwd_in.at[d - 1], 34 + d, y_dev(d)) for d in range(1, 4)]
@@ -379,7 +383,14 @@
     m6, m7 = unfar(fwd_mean(2, 0), fwd_mean(2, 1))
     for chunk, row in enumerate((fwd_mean(0, 0), fwd_mean(0, 1), fwd_mean(3, 0), fwd_mean(1, 1),
                                  fwd_mean(3, 1), fwd_mean(1, 0), m6, m7)):
-        fcol[chunk * 128:(chunk + 1) * 128, :] = jnp.transpose(jnp.broadcast_to(row, (128, 128)))
+        rowform[chunk] = row
+
+    def spread(chunk, _):
+        at = pl.ds(aligned(chunk * 128, 128), 128)
+        fcol[at, :] = jnp.transpose(jnp.broadcast_to(rowform[chunk], (128, 128)))
+        return 0
+
+    lax.fori_loop(0, 8, spread, 0)
 
     for copy in bwd_x:
         copy.wait_recv()
@@ -405,24 +416,23 @@
         put_brow(14 + p, distant)
 
     def margins(chunks, unroll, first):
-        peaks = (jnp.zeros((8, 128), F32),) * len(chunks)
-        for chunk_row in range(8):
-            rel = ROW_REL[chunk_row]
-
-            def margin_rows(g, peaks):
-                at = pl.ds(aligned(chunk_row * 128 + g * 8, 8), 8)
+        def margin_rows(step, peaks):
+            peaks = list(peaks)
+            kind = step // (16 // unroll)
+            for g in range(unroll):
+                at = pl.ds(aligned(step * (8 * unroll) + g * 8, 8), 8)
                 mean = fcol[at, :]
                 best = jnp.zeros((8, 128), F32) if first else fwd_val[at, :]
-                new = []
-                for peak, chunk in zip(peaks, chunks):
+                for i, chunk in enumerate(chunks):
                     cols = slice(chunk * 128, (chunk + 1) * 128)
-                    margin = (scores[at, cols] * weight[rel, :, cols]) / (mean + brow[:, cols])
+                    margin = (scores[at, cols] * weight[kind, :, cols]) / (mean + brow[:, cols])
                     best = jnp.maximum(best, margin)
-                    new.append(jnp.maximum(peak, margin))
+                    peaks[i] = jnp.maximum(peaks[i], margin)
                 fwd_val[at, :] = best
-                return tuple(new)
-
-            peaks = lax.fori_loop(0, 16, margin_rows, peaks, unroll=unroll)
+            return tuple(peaks)
+
+        peaks = lax.fori_loop(0, 128 // unroll, margin_rows,
+                              (jnp.zeros((8, 128), F32),) * len(chunks))
         return {chunk: jnp.max(peak, axis=0, keepdims=True) for chunk, peak in zip(chunks, peaks)}
 
     def put_peaks(peaks):
@@ -448,11 +458,8 @@
         copy.start()
     tgt_copies += own_sends
 
-    def src_peak(chunk):
-        values = jnp.transpose(fwd_val[chunk * 128:(chunk + 1) * 128, :])
-        return jnp.max(values, axis=0, keepdims=True)
-
-    for rel, rows in enumerate(natural_rows(src_peak)):
+    to_rows(lambda values: jnp.max(values, axis=0, keepdims=True))
+    for rel, rows in enumerate(natural_rows(row_of)):
         for i, value in enumerate(rows):
             src_part[lax.rem(y + rel, 4), i:i + 1, :] = value
     src_y = [remote(src_part.at[lax.rem(y + d, 4)], src_in.at[d - 1], 56 + d, y_dev(d))
@@ -497,8 +504,8 @@
             pltpu.VMEM((16, 1024), I32), pltpu.VMEM((4, 16, 512), I32),
             pltpu.VMEM((1024, 128), I32), pltpu.VMEM((16, 2048), I32),
             pltpu.VMEM((1024, 128), F32), pltpu.VMEM((16, 2048), F32),
-            pltpu.VMEM((4, 1, 2048), F32),
-            pltpu.VMEM((4, 2, 128), F32), pltpu.VMEM((1024, 128), F32),
+            pltpu.VMEM((8, 1, 2048), F32),
+            pltpu.VMEM((4, 2, 128), F32), pltpu.VMEM((8, 1, 128), F32), pltpu.VMEM((1024, 128), F32),
             pltpu.VMEM((1, 2048), F32),
             pltpu.VMEM((4, 2, 128), F32), pltpu.VMEM((3, 4, 2, 128), F32),
             pltpu.VMEM((4, 4, 128), F32), pltpu.VMEM((7, 4, 4, 128), F32),

time: 51.3 us -> 50.8 us (level)
  no operation moved by 1% of the time
where the time goes in v5:
time: 50.8 us; the launch traced here: 50.6 us
  Pallas kernels  50 us (98%)
  between operations  0.64 us (1%)
    pallas_call x1, Pallas kernels, body(): pl.pallas_call(kernel, out_shape=(jax.ShapeDtypeStruct((2, 128), F32), ja...  48.7 us
    pallas_call x1, Pallas kernels, body(): pl.pallas_call(flatten, out_shape=(jax.ShapeDtypeStruct((256,), F32), jax...  1.27 us

profile of v5, /device:TPU:1, one launch (start us, length us, event | category | flops | bytes accessed | tf_op | source)
XLA Modules:
  0.0 50.6 jit_solution(11126661438315268717)
XLA Ops:
  0.6 48.7 %shard_map.68 = (f32[2,128]{1,0:T(2,128)}, f32[4,128]{1,0:T(4,128)}) custom-call(bf16[256,1024]{1,0:T(8,128)(2,1)} %src_hbm.1, bf16[512,1024]{1,0:T(8,128)(2,1)} %tgt_hbm.1, s32[8,16]{1,0:T(8,128)} %bitcast.5, s32[16,4096]{1,0:T(8,128)} %bitcast.3, s32[16,512]{1,0:T(8,128)} %bitcast.4), custom_call_target="tpu_custom_call" | custom-call | tf_op jit(solution)/shard_map/pallas_call | solution.py:494
  49.3 1.3 %shard_map.69 = (f32[256]{0:T(256)}, f32[512]{0:T(512)}) custom-call(f32[2,128]{1,0:T(2,128)} %get-tuple-element.4.src_ref, f32[4,128]{1,0:T(4,128)} %get-tuple-element.5.tgt_ref), custom_call_target="tpu_custom_call" | custom-call | tf_op jit(solution)/shard_map/pallas_call | solution.py:528

commit v6 on v5

--- a/solution.py
+++ b/solution.py
@@ -103,8 +103,6 @@
     for copy in own_copies[:4]:
         copy.start()
     for copy in idx_copies[:2]:
-        copy.start()
-    for copy in own_copies[4:]:
         copy.start()
     for device in (zc_dev(2), zc_dev(6)):
         pl.semaphore_signal(ready_sem, inc=1, device_id=device, device_id_type=MESH)
@@ -229,6 +227,8 @@
                 fwd_val[at, :] = value
 
     region(0, 256, 0, 512)
+    for copy in own_copies[4:]:
+        copy.start()
 
     for copy in own_copies[:4] + idx_copies[:2]:
         copy.wait_recv()
@@ -243,7 +243,7 @@
         remote(trow(576 + c256, 64), trow(1856 + c128, 64), 17, x_dev(1)),
         remote(trow(640 + c256, 64), trow(1792 + c128, 64), 18, x_dev(3)),
     )
-    for copy in far_copies:
+    for copy in far_copies[:4]:
         copy.start()
     pl.semaphore_wait(ready_sem, 2)
     partner = zc_dev(1)
@@ -274,6 +274,8 @@
         bwd_put(9 + 2 * p, bwd_half(1, p, 0))
     pass_copies[0].wait_recv()
     region(0, 512, 512, 512)
+    for copy in far_copies[4:]:
+        copy.start()
 
     for copy in own_copies[4:] + idx_copies[2:]:
         copy.wait_recv()
@@ -296,14 +298,13 @@
     pass_copies[3].wait_recv()
     region(0, 768, 1536, 256)
 
-    for copy in far_copies[:2] + far_copies[4:6]:
-        copy.wait_recv()
-    region(768, 256, 0, 768)
     far_copies[6].wait_recv()
     pass_copies[4].start()
     far_copies[7].wait_recv()
     pass_copies[5].start()
-    region(768, 256, 768, 1024)
+    for copy in far_copies[:2] + far_copies[4:6]:
+        copy.wait_recv()
+    region(768, 256, 0, 1792)
     pass_copies[4].wait_recv()
     pass_copies[5].wait_recv()
     region(0, 1024, 1792, 256)

time: 50.8 us -> 50.1 us (0.986)
  Pallas kernels: 50 us -> 49.3 us
    pallas_call x1, Pallas kernels: 48.7 us -> 48.1 us  [body(): pl.pallas_call(kernel, out_shape=(jax.ShapeDtypeStruct((2, 128), F32), ja...]
where the time goes in v6:
time: 50.1 us; the launch traced here: 50 us
  Pallas kernels  49.3 us (98%)
  between operations  0.64 us (1%)
    pallas_call x1, Pallas kernels, body(): pl.pallas_call(kernel, out_shape=(jax.ShapeDtypeStruct((2, 128), F32), ja...  48.1 us
    pallas_call x1, Pallas kernels, body(): pl.pallas_call(flatten, out_shape=(jax.ShapeDtypeStruct((256,), F32), jax...  1.27 us

profile of v6, /device:TPU:1, one launch (start us, length us, event | category | flops | bytes accessed | tf_op | source)
XLA Modules:
  0.0 50.0 jit_solution(4751165485076546060)
XLA Ops:
  0.6 48.1 %shard_map.68 = (f32[2,128]{1,0:T(2,128)}, f32[4,128]{1,0:T(4,128)}) custom-call(bf16[256,1024]{1,0:T(8,128)(2,1)} %src_hbm.1, bf16[512,1024]{1,0:T(8,128)(2,1)} %tgt_hbm.1, s32[8,16]{1,0:T(8,128)} %bitcast.5, s32[16,4096]{1,0:T(8,128)} %bitcast.3, s32[16,512]{1,0:T(8,128)} %bitcast.4), custom_call_target="tpu_custom_call" | custom-call | tf_op jit(solution)/shard_map/pallas_call | solution.py:495
  48.7 1.3 %shard_map.69 = (f32[256]{0:T(256)}, f32[512]{0:T(512)}) custom-call(f32[2,128]{1,0:T(2,128)} %get-tuple-element.4.src_ref, f32[4,128]{1,0:T(4,128)} %get-tuple-element.5.tgt_ref), custom_call_target="tpu_custom_call" | custom-call | tf_op jit(solution)/shard_map/pallas_call | solution.py:529
